TPU v7x, 256 devices: a whole 4x4x8 slice. The times are simulated.
256 devices in a mesh: blk: 8 (over y, core), wide: 8 (over z), dp: 4 (over x).
Axes of the slice: x: 4, y: 4, z: 8, core: 2. Of those that a mesh axis runs over, the one named last changes fastest.
Arguments:
- token_ids: int32 [32768], P(('dp', 'blk', 'wide')), parts along dimension 0, may hold values from 0 to 5
- embedding: float32 [6, 1536], replicated, may hold values from -3 to 3
- queries: bfloat16 [32768, 768], P(('dp', 'blk', 'wide')), parts along dimension 0, may hold values from -12 to 12
- key_rows: bfloat16 [32768, 768], P(('dp', 'blk', 'wide')), parts along dimension 0, may hold values from -6 to 6
- value_rows: bfloat16 [32768, 768], P(('dp', 'blk', 'wide')), parts along dimension 0, may hold values from -6 to 6
- head_mixer: bfloat16 [768, 1536], replicated, may hold values from -0.21875 to 0.21875
- expand_weight: bfloat16 [1536, 3072], P(None, 'wide'), may hold values from -0.15625 to 0.15625
- reduce_weight: bfloat16 [3072, 1536], P('wide'), may hold values from -0.109375 to 0.109375
- cotangent: bfloat16 [32768, 1536], P(('dp', 'blk', 'wide')), parts along dimension 0, may hold values from -0.29882812 to 0.29882812
Outputs:
- restored: bfloat16 [32768, 1536], P(('dp', 'blk', 'wide')), parts along dimension 0
- expand_grad: float32 [6144, 3072], P(('dp', 'blk'), 'wide'), parts along dimension 0
- reduce_grad: float32 [12288, 1536], P(('dp', 'wide'), 'blk'), parts along dimension 0
There are 4 independent parts, one for each index of `dp`. A program takes and returns all parts, laid end to end along the dimension named above; an argument that names none is the same for every part. Nothing has to cross between parts.
All inputs are finite; a program needn't handle non-finite values.
Results may differ from a plain program's by a relative error of at most 0.018.
Values may be sent and summed in bfloat16 or wider, within the bound.
A program may use at most 128 MiB of HBM per device.

v0:
```python
import jax
import jax.numpy as jnp
from jax import lax
from jax.sharding import PartitionSpec as P

FINE_HEADS = 6
HEAD = 128
VOCAB = 6
POOL = 8


NEGATIVE = -1e30


def side_by_side(arrays, axis, dim, along):
    widths = [a.shape[along] for a in arrays]
    both = jnp.concatenate(arrays, axis=along)
    result = lax.all_gather(both, axis, axis=dim, tiled=True)
    return tuple(jnp.split(result, [sum(widths[:k]) for k in range(1, len(widths))], axis=along))


def from_behind(array, axis, by):
    size = lax.axis_size(axis)
    pairs = [(i, i + by) for i in range(size) if 0 <= i + by < size]
    return lax.ppermute(array, axis, pairs)


def in_order(blocks, dim):
    shape = list(blocks.shape[1:])
    shape[dim] *= blocks.shape[0]
    return jnp.moveaxis(blocks, 0, dim).reshape(shape)


def copy_for_each(array, axis):
    copies = jnp.broadcast_to(array, (lax.axis_size(axis), *array.shape))
    return lax.all_to_all(copies, axis, split_axis=0, concat_axis=0, tiled=True)


def gather_directly(array, axis, dim):
    return in_order(copy_for_each(array, axis), dim)


def in_blocks(array, dim, size):
    before, after = (array.shape[:dim], array.shape[dim + 1 :])
    return jnp.moveaxis(array.reshape(*before, size, -1, *after), dim, 0)


def sum_at_owner(array, axis, dim):
    blocks = in_blocks(array, dim, lax.axis_size(axis))
    arrived = lax.all_to_all(blocks, axis, split_axis=0, concat_axis=0, tiled=True)
    return arrived.astype(jnp.float32).sum(axis=0)


def empty_state(query_count):
    return (
        jnp.full((FINE_HEADS, query_count), NEGATIVE, jnp.float32),
        jnp.zeros((FINE_HEADS, query_count), jnp.float32),
        jnp.zeros((FINE_HEADS, query_count, HEAD), jnp.float32),
    )


def attend(fold_state, query_block, query_position, key_block, value_block, key_position):
    maxima, totals, summed = fold_state
    query_count = query_block.shape[0]
    key_count = key_block.shape[0]
    query_heads = query_block.reshape(query_count, FINE_HEADS, HEAD)
    key_heads = key_block.reshape(key_count, FINE_HEADS, HEAD)
    value_heads = value_block.reshape(key_count, FINE_HEADS, HEAD)
    scores = jnp.einsum(
        "rhd,khd->hrk", query_heads, key_heads, preferred_element_type=jnp.float32
    ) * HEAD ** (-0.5)
    allowed = (key_position[None, :] <= query_position[:, None])[None]
    scores = jnp.where(allowed, scores, NEGATIVE)
    highest = jnp.maximum(maxima, scores.max(-1))
    weights = jnp.where(allowed, jnp.exp(scores - highest[..., None]), 0.0)
    factor = jnp.exp(maxima - highest)
    totals = totals * factor + weights.sum(-1)
    summed = summed * factor[..., None] + jnp.einsum(
        "hrk,khd->hrd",
        weights.astype(jnp.bfloat16),
        value_heads,
        preferred_element_type=jnp.float32,
    )
    return (highest, totals, summed)


def finish(fold_state):
    maxima, totals, summed = fold_state
    result = summed / totals[..., None]
    return result.transpose(1, 0, 2).reshape(summed.shape[1], -1).astype(jnp.bfloat16)


def key_block_rows():
    return 512


def local(
    token_ids,
    embedding,
    queries,
    key_rows,
    value_rows,
    head_mixer,
    expand_weight,
    reduce_weight,
    cotangent,
):
    shard_rows = queries.shape[0]
    self_index = lax.axis_index(("blk", "wide"))
    query_position = self_index * shard_rows + jnp.arange(shard_rows, dtype=jnp.int32)
    last_position = self_index * shard_rows + shard_rows - 1
    key_piece, value_piece = side_by_side((key_rows, value_rows), ("blk", "wide"), 0, 1)
    block_rows = key_block_rows()

    def step(block_index, carry_state):
        offset = block_index * block_rows
        key_block = lax.dynamic_slice_in_dim(key_piece, offset, block_rows, 0)
        value_block = lax.dynamic_slice_in_dim(value_piece, offset, block_rows, 0)
        key_position = offset + jnp.arange(block_rows, dtype=jnp.int32)
        return lax.cond(
            offset <= last_position,
            lambda current: attend(
                current, queries, query_position, key_block, value_block, key_position
            ),
            lambda current: current,
            carry_state,
        )

    attended = finish(
        lax.fori_loop(0, key_piece.shape[0] // block_rows, step, empty_state(shard_rows))
    )
    onehot = (token_ids[:, None] == jnp.arange(VOCAB, dtype=jnp.int32)[None, :]).astype(jnp.float32)
    stream = jnp.dot(
        onehot, embedding, precision=lax.Precision.HIGHEST, preferred_element_type=jnp.float32
    )
    stream = stream + jnp.dot(attended, head_mixer, preferred_element_type=jnp.float32)
    carried = from_behind(stream[-1:], ("blk", "wide"), 1)
    shifted = jnp.concatenate([carried, stream[:-1]], 0)
    pooled = shifted.reshape(-1, POOL, stream.shape[1]).mean(axis=1).astype(jnp.bfloat16)
    pooled_wide = gather_directly(pooled, "wide", 0)
    pooled_float = pooled_wide.astype(jnp.float32)
    normed = (
        pooled_float * lax.rsqrt(jnp.mean(pooled_float * pooled_float, -1, keepdims=True) + 1e-06)
    ).astype(jnp.bfloat16)
    expanded = jnp.dot(normed, expand_weight, preferred_element_type=jnp.float32)
    activated = jax.nn.gelu(expanded).astype(jnp.bfloat16)
    middle = pooled.astype(jnp.float32) + sum_at_owner(
        jnp.dot(activated, reduce_weight, preferred_element_type=jnp.float32).astype(jnp.bfloat16),
        "wide",
        0,
    )
    earlier = from_behind(middle[-1:], ("blk", "wide"), 1)
    before = jnp.concatenate([earlier, middle[:-1]], 0)
    steps_index = jnp.arange(POOL, dtype=jnp.float32)
    after_weights = (steps_index + 1.0) / POOL
    before_weights = (POOL - 1.0 - steps_index) / POOL
    upsampled = (
        middle[:, None, :] * after_weights[None, :, None]
        + before[:, None, :] * before_weights[None, :, None]
    ).reshape(stream.shape)
    restored = (stream + upsampled).astype(jnp.bfloat16)
    grad_rows = cotangent.astype(jnp.float32).reshape(-1, POOL, stream.shape[1])
    own_part = jnp.einsum("sid,i->sd", grad_rows, after_weights)
    later_part = jnp.einsum("sid,i->sd", grad_rows, before_weights)
    following = from_behind(later_part[:1], ("blk", "wide"), -1)
    middle_grad = (own_part + jnp.concatenate([later_part[1:], following], 0)).astype(jnp.bfloat16)
    grad_wide = gather_directly(middle_grad, "wide", 0)
    act_grad = lax.dot_general(
        grad_wide, reduce_weight, (((1,), (1,)), ((), ())), preferred_element_type=jnp.float32
    )
    pre_grad = jax.vjp(jax.nn.gelu, expanded)[1](act_grad)[0].astype(jnp.bfloat16)
    normed_cols, grad_cols = (
        lax.all_to_all(normed, "blk", split_axis=1, concat_axis=0, tiled=True),
        lax.all_to_all(grad_wide, "blk", split_axis=1, concat_axis=0, tiled=True),
    )
    pre_all, act_all = side_by_side((pre_grad, activated), "blk", 0, 1)
    expand_grad = jnp.einsum("gi,gj->ij", normed_cols, pre_all, preferred_element_type=jnp.float32)
    reduce_grad = jnp.einsum("gi,gj->ij", act_all, grad_cols, preferred_element_type=jnp.float32)
    return (restored, expand_grad, reduce_grad)


def solution(mesh):
    return jax.shard_map(
        local,
        mesh=mesh,
        in_specs=(
            P(("dp", "blk", "wide")),
            P(),
            P(("dp", "blk", "wide"), None),
            P(("dp", "blk", "wide"), None),
            P(("dp", "blk", "wide"), None),
            P(),
            P(None, "wide"),
            P("wide", None),
            P(("dp", "blk", "wide"), None),
        ),
        out_specs=(
            P(("dp", "blk", "wide"), None),
            P(("dp", "blk"), "wide"),
            P(("dp", "wide"), "blk"),
        ),
        check_vma=False,
    )
```

profile of v0, /device:TPU:1, one launch (start us, length us, event | category | flops | bytes accessed | tf_op | source)
XLA Modules:
  0.0 314.6 jit_solution(15438838187839720245)
XLA Ops:
  7.3 1.2 copy.28
  8.5 1.1 copy.29
  9.6 0.8 pad_maximum_fusion
  10.6 1.4 fusion.34
  12.0 133.3 %all-gather.3.cloned.1.call-done = bf16[8192,1536]{0,1:T(8,128)(2,1)} async-done(((bf16[128,1536]{0,1:T(8,128)(2,1)}), bf16[8192,1536]{0,1:T(8,128)(2,1)}) %all-gather.3.cloned.1.call-update) | async-done | bytes 25165840 | tf_op jit(solution)/shard_map/all_gather | solution.py:18
  145.3 17.3 %fusion.43 = (bf16[8192,768]{0,1:T(8,128)(2,1)}, bf16[8192,768]{0,1:T(8,128)(2,1)}) fusion(bf16[8192,1536]{0,1:T(8,128)(2,1)} %all-gather.3.cloned.1.call-done), kind=kLoop, calls=%fused_computation.75 | loop fusion | bytes 50331648 | tf_op jit(solution)/shard_map/split | solution.py:19
  162.7 10.3 %while.18 = (s32[]{:T(128)}, f32[6,128]{1,0:T(8,128)S(1)}, f32[6,128]{1,0:T(8,128)S(1)}, f32[6,128,128]{2,1,0:T(8,128)S(1)}, s32[]{:T(128)}, /*index=5*/bf16[819...) while((s32[]{:T(128)}, f32[6,128]{1,0:T(8,128)S(1)}, ...), condition=%wide.region_5.6_spmd.clone, body=%wide.region_0.5_spmd.clone.sunk | while | flops 205129856 | bytes 10742077 | solution.py:130
  162.7 3.1 conditional.3
  162.7 1.5 constant_dynamic-slice_fusion
  165.2 0.6 convolution_add_fusion
  165.9 3.1 conditional.3
  165.9 1.5 constant_dynamic-slice_fusion
  169.0 3.1 conditional.3
  169.1 1.5 constant_dynamic-slice_fusion
  173.2 1.7 convolution_add_fusion.1
  174.9 2.3 collective-permute-start
  177.5 4.5 %collective-permute-start.2 = (f32[1,1536]{1,0:T(1,128)S(1)}, f32[1,1536]{1,0:T(1,128)S(1)}, u32[]{:S(2)}, u32[]{:S(2)}) collective-permute-start(f32[1,1536]{1,0:T(1,128)S(1)} %slice.29), channel_id=1, source_target_pairs={{4,0},{8,4},{12,8},{16,12},{20,16},{24,20},{28,24},{32,28},{36,32}... | collective-permute-start | bytes 18440 | tf_op jit(solution)/shard_map/ppermute | solution.py:25
  182.4 0.6 copy-done.2
  183.0 0.8 broadcast_in_dim.59
  183.8 7.3 %all-to-all-start = ((bf16[8,16,1536]{2,1,0:T(8,128)(2,1)}), bf16[8,16,1536]{2,1,0:T(8,128)(2,1)S(1)}, u32[]{:S(2)}, u32[]{:S(2)}) async-start(bf16[8,16,1536]{2,1,0:T(8,128)(2,1)} %broadcast_in_dim.59), calls=%async_computation | async-start | bytes 786432 | tf_op jit(solution)/shard_map/all_to_all | solution.py:36
  191.1 1.2 fusion.24
  192.3 0.9 slice.28
  193.3 0.6 fusion.33
  193.9 7.9 %all-to-all-done = bf16[8,16,1536]{2,1,0:T(8,128)(2,1)S(1)} async-done(((bf16[8,16,1536]{2,1,0:T(8,128)(2,1)}), bf16[8,16,1536]{2,1,0:T(8,128)(2,1)S(1)}, u32[]{:S(2)}, u32[]{:S(2)}) %all-to-all-start) | async-done | bytes 393248 | tf_op jit(solution)/shard_map/all_to_all | solution.py:36
  201.8 1.6 broadcast_in_dim.60
  203.4 4.1 %all-to-all-start.3 = ((bf16[8,16,1536]{2,1,0:T(8,128)(2,1)}), bf16[8,16,1536]{2,1,0:T(8,128)(2,1)}, u32[]{:S(2)}, u32[]{:S(2)}) async-start(bf16[8,16,1536]{2,1,0:T(8,128)(2,1)} %broadcast_in_dim.60), calls=%async_computation.3 | async-start | bytes 786432 | tf_op jit(solution)/shard_map/all_to_all | solution.py:36
  208.0 2.3 fusion.44
  210.3 8.3 %all-to-all-done.3 = bf16[8,16,1536]{2,1,0:T(8,128)(2,1)} async-done(((bf16[8,16,1536]{2,1,0:T(8,128)(2,1)}), bf16[8,16,1536]{2,1,0:T(8,128)(2,1)}, u32[]{:S(2)}, u32[]{:S(2)}) %all-to-all-start.3) | async-done | bytes 393248 | tf_op jit(solution)/shard_map/all_to_all | solution.py:36
  218.6 1.9 fusion.32
  220.6 0.6 copy-done.4
  221.2 0.7 pad_maximum_fusion.1
  221.9 2.4 convolution_convert_fusion
  224.4 4.1 %all-to-all-start.1 = ((bf16[8,16,1536]{2,1,0:T(8,128)(2,1)}), bf16[8,16,1536]{2,1,0:T(8,128)(2,1)}, u32[]{:S(2)}, u32[]{:S(2)}) async-start(bf16[8,16,1536]{2,1,0:T(8,128)(2,1)} %bitcast.80), calls=%async_computation.1 | async-start | bytes 786432 | tf_op jit(solution)/shard_map/all_to_all | solution.py:50
  229.2 2.3 all_to_all.41
  231.5 2.2 copy.34
  233.7 1.3 reshape.133
  235.0 6.4 %all-to-all-done.1 = bf16[8,16,1536]{2,1,0:T(8,128)(2,1)} async-done(((bf16[8,16,1536]{2,1,0:T(8,128)(2,1)}), bf16[8,16,1536]{2,1,0:T(8,128)(2,1)}, u32[]{:S(2)}, u32[]{:S(2)}) %all-to-all-start.1) | async-done | bytes 393248 | tf_op jit(solution)/shard_map/all_to_all | solution.py:50
  241.4 42.3 %all-to-all-start.4 = ((bf16[128,8,192]{0,2,1:T(8,128)(2,1)}), bf16[128,8,192]{0,2,1:T(8,128)(2,1)}, u32[]{:S(2)}, u32[]{:S(2)}) async-start(bf16[128,8,192]{0,2,1:T(8,128)(2,1)} %copy.34), calls=%async_computation.4 | async-start | bytes 786432 | tf_op jit(solution)/shard_map/all_to_all | solution.py:174
  283.8 1.1 convert_reduce_fusion
  284.8 0.9 convert_add_fusion
  285.8 2.1 collective-permute-start.1
  287.9 2.2 multiply_convert_fusion
  290.1 2.2 copy.32
  292.4 5.3 %all-to-all-start.2 = ((bf16[128,8,192]{0,2,1:T(8,128)(2,1)}), bf16[128,8,192]{0,2,1:T(8,128)(2,1)}, u32[]{:S(2)}, u32[]{:S(2)}) async-start(bf16[128,8,192]{0,2,1:T(8,128)(2,1)} %copy.32), calls=%async_computation.2 | async-start | bytes 786432 | tf_op jit(solution)/shard_map/all_to_all | solution.py:173
  297.7 0.9 fusion.16
  298.6 2.3 fusion.9
  300.9 4.5 %all-to-all-done.2 = bf16[128,8,192]{0,2,1:T(8,128)(2,1)} async-done(((bf16[128,8,192]{0,2,1:T(8,128)(2,1)}), bf16[128,8,192]{0,2,1:T(8,128)(2,1)}, u32[]{:S(2)}, u32[]{:S(2)}) %all-to-all-start.2) | async-done | bytes 393248 | tf_op jit(solution)/shard_map/all_to_all | solution.py:173
  305.5 2.3 fusion.11
  (120 shorter events, 6.5 us)
Async XLA Ops:
  7.2 166.0 %copy-start = (bf16[768,1536]{1,0:T(8,128)(2,1)S(1)}, bf16[768,1536]{1,0:T(8,128)(2,1)}, u32[]{:S(2)}) copy-start(bf16[768,1536]{1,0:T(8,128)(2,1)} %param.18) | copy-start | bytes 7077892
  7.2 3.2 %copy-start.5 = (bf16[128,768]{1,0:T(8,128)(2,1)S(1)}, bf16[128,768]{1,0:T(8,128)(2,1)}, u32[]{:S(2)}) copy-start(bf16[128,768]{1,0:T(8,128)(2,1)} %param.15) | copy-start | bytes 589828
  7.2 3.4 %copy-start.8 = (s32[128]{0:T(128)S(1)}, s32[128]{0:T(128)}, u32[]{:S(2)}) copy-start(s32[128]{0:T(128)} %param.13) | copy-start | bytes 1540
  7.2 3.4 %copy-start.6 = (f32[6,1536]{1,0:T(8,128)S(1)}, f32[6,1536]{1,0:T(8,128)}, u32[]{:S(2)}) copy-start(f32[6,1536]{1,0:T(8,128)} %param.14) | copy-start | bytes 110596
  7.2 138.1 %all-gather.3.cloned.1.call-start = ((), (), s32[]{:S(2)}) async-start(), calls=%async_computation.5 | async-start | bytes 25559040 | tf_op jit(solution)/shard_map/all_gather | solution.py:18
  173.2 4.0 %copy-start.1 = (bf16[128,1536]{1,0:T(8,128)(2,1)S(1)}, bf16[128,1536]{1,0:T(8,128)(2,1)}, u32[]{:S(2)}) copy-start(bf16[128,1536]{1,0:T(8,128)(2,1)} %param.21) | copy-start | bytes 1179652
  174.9 7.1 %collective-permute-start = (f32[1,1536]{1,0:T(1,128)S(1)}, f32[1,1536]{1,0:T(1,128)S(1)}, u32[]{:S(2)}, u32[]{:S(2)}) collective-permute-start(f32[1,1536]{1,0:T(1,128)S(1)} %slice.24), channel_id=1, source_target_pairs={{0,4},{4,8},{8,12},{12,16},{16,20},{20,24},{24,28},{28,32},{32,36}... | collective-permute-start | bytes 18440 | tf_op jit(solution)/shard_map/ppermute | solution.py:25
  177.5 4.5 %copy-start.3 = (f32[1,16,1536]{2,1,0:T(8,128)}, f32[1,16,1536]{2,1,0:T(8,128)S(1)}, u32[]{:S(2)}) copy-start(f32[1,16,1536]{2,1,0:T(8,128)S(1)} %copy.54) | copy-start | bytes 294916
  177.5 15.7 %collective-permute-start.2 = (f32[1,1536]{1,0:T(1,128)S(1)}, f32[1,1536]{1,0:T(1,128)S(1)}, u32[]{:S(2)}, u32[]{:S(2)}) collective-permute-start(f32[1,1536]{1,0:T(1,128)S(1)} %slice.29), channel_id=1, source_target_pairs={{4,0},{8,4},{12,8},{16,12},{20,16},{24,20},{28,24},{32,28},{36,32}... | collective-permute-start | bytes 18440 | tf_op jit(solution)/shard_map/ppermute | solution.py:25
  182.4 0.6 copy-start.2
  183.8 18.1 %all-to-all-start = ((bf16[8,16,1536]{2,1,0:T(8,128)(2,1)}), bf16[8,16,1536]{2,1,0:T(8,128)(2,1)S(1)}, u32[]{:S(2)}, u32[]{:S(2)}) async-start(bf16[8,16,1536]{2,1,0:T(8,128)(2,1)} %broadcast_in_dim.59), calls=%async_computation | async-start | bytes 786432 | tf_op jit(solution)/shard_map/all_to_all | solution.py:36
  203.4 15.2 %all-to-all-start.3 = ((bf16[8,16,1536]{2,1,0:T(8,128)(2,1)}), bf16[8,16,1536]{2,1,0:T(8,128)(2,1)}, u32[]{:S(2)}, u32[]{:S(2)}) async-start(bf16[8,16,1536]{2,1,0:T(8,128)(2,1)} %broadcast_in_dim.60), calls=%async_computation.3 | async-start | bytes 786432 | tf_op jit(solution)/shard_map/all_to_all | solution.py:36
  207.5 91.1 %all-gather.5.cloned.1.call-start = ((), (), s32[]{:S(2)}) async-start(), calls=%async_computation.6 | async-start | bytes 1769472 | tf_op jit(solution)/shard_map/all_gather | solution.py:18
  220.6 0.6 copy-start.4
  224.4 17.1 %all-to-all-start.1 = ((bf16[8,16,1536]{2,1,0:T(8,128)(2,1)}), bf16[8,16,1536]{2,1,0:T(8,128)(2,1)}, u32[]{:S(2)}, u32[]{:S(2)}) async-start(bf16[8,16,1536]{2,1,0:T(8,128)(2,1)} %bitcast.80), calls=%async_computation.1 | async-start | bytes 786432 | tf_op jit(solution)/shard_map/all_to_all | solution.py:50
  241.4 50.9 %all-to-all-start.4 = ((bf16[128,8,192]{0,2,1:T(8,128)(2,1)}), bf16[128,8,192]{0,2,1:T(8,128)(2,1)}, u32[]{:S(2)}, u32[]{:S(2)}) async-start(bf16[128,8,192]{0,2,1:T(8,128)(2,1)} %copy.34), calls=%async_computation.4 | async-start | bytes 786432 | tf_op jit(solution)/shard_map/all_to_all | solution.py:174
  285.7 11.9 %copy-start.7 = (f32[128]{0:T(128)S(1)}, f32[128]{0:T(128)}, u32[]{:S(2)}) copy-start(f32[128]{0:T(128)} %mul.165) | copy-start | bytes 1540
  285.8 6.6 %collective-permute-start.1 = (f32[1,1536]{1,0:T(1,128)S(1)}, f32[1,1536]{1,0:T(1,128)S(1)}, u32[]{:S(2)}, u32[]{:S(2)}) collective-permute-start(f32[1,1536]{1,0:T(1,128)S(1)} %slice.26), channel_id=1, source_target_pairs={{0,4},{4,8},{8,12},{12,16},{16,20},{20,24},{24,28},{28,32},{32,36}... | collective-permute-start | bytes 18440 | tf_op jit(solution)/shard_map/ppermute | solution.py:25
  292.4 13.1 %all-to-all-start.2 = ((bf16[128,8,192]{0,2,1:T(8,128)(2,1)}), bf16[128,8,192]{0,2,1:T(8,128)(2,1)}, u32[]{:S(2)}, u32[]{:S(2)}) async-start(bf16[128,8,192]{0,2,1:T(8,128)(2,1)} %copy.32), calls=%async_computation.2 | async-start | bytes 786432 | tf_op jit(solution)/shard_map/all_to_all | solution.py:173
Sparse Core Ops, SparseCore 0:
  11.1 134.1 all-gather.2
  222.0 60.0 all-gather.4
where the time goes:
time: 316 us; the launch traced here: 315 us
  waiting for transfers between devices  161 us (51%)
  starting transfers between devices  72.1 us (23%)
  local copies, waits for them, and re-layouts  37.9 us (12%)
  matrix products  19.2 us (6%)
  between operations  14.4 us (5%)
  other arithmetic  9.26 us (3%)
    all_gather x2, waiting for transfers between devices, side_by_side(): result = lax.all_gather(both, axis, axis=dim, tiled=True)  133 us
    all_to_all x1, starting transfers between devices, local(): lax.all_to_all(grad_wide, 'blk', split_axis=1, concat_axis=0, tiled=True)  42.3 us
    split x1, local copies, waits for them, and re-layouts, side_by_side(): jnp.split(result, [sum(widths[:k]) for k in range(1, len(widths))], axis=...  17.3 us
    all_to_all x2, waiting for transfers between devices, copy_for_each(): return lax.all_to_all(copies, axis, split_axis=0, concat_axis=0, tiled=True)  16.3 us
    all_to_all x2, starting transfers between devices, copy_for_each(): return lax.all_to_all(copies, axis, split_axis=0, concat_axis=0, tiled=True)  11.4 us
    ppermute x3, starting transfers between devices, from_behind(): return lax.ppermute(array, axis, pairs)  8.88 us
    all_to_all x1, waiting for transfers between devices, sum_at_owner(): lax.all_to_all(blocks, axis, split_axis=0, concat_axis=0, tiled=True)  6.44 us
  transfers between devices with their start and end apart: 10, of which 5 were waited for; matrix products, arithmetic and copies ran while one was open for 8% of the time, Pallas kernels for 0%

commit v1 on v0

--- a/solution.py
+++ b/solution.py
@@ -1,15 +1,14 @@
 import jax
 import jax.numpy as jnp
 from jax import lax
+from jax.experimental import pallas as pl
+from jax.experimental.pallas import tpu as pltpu
 from jax.sharding import PartitionSpec as P
 
 FINE_HEADS = 6
 HEAD = 128
 VOCAB = 6
 POOL = 8
-
-
-NEGATIVE = -1e30
 
 
 def side_by_side(arrays, axis, dim, along):
@@ -51,47 +50,320 @@
     return arrived.astype(jnp.float32).sum(axis=0)
 
 
-def empty_state(query_count):
-    return (
-        jnp.full((FINE_HEADS, query_count), NEGATIVE, jnp.float32),
-        jnp.zeros((FINE_HEADS, query_count), jnp.float32),
-        jnp.zeros((FINE_HEADS, query_count, HEAD), jnp.float32),
-    )
-
-
-def attend(fold_state, query_block, query_position, key_block, value_block, key_position):
-    maxima, totals, summed = fold_state
-    query_count = query_block.shape[0]
-    key_count = key_block.shape[0]
-    query_heads = query_block.reshape(query_count, FINE_HEADS, HEAD)
-    key_heads = key_block.reshape(key_count, FINE_HEADS, HEAD)
-    value_heads = value_block.reshape(key_count, FINE_HEADS, HEAD)
-    scores = jnp.einsum(
-        "rhd,khd->hrk", query_heads, key_heads, preferred_element_type=jnp.float32
-    ) * HEAD ** (-0.5)
-    allowed = (key_position[None, :] <= query_position[:, None])[None]
-    scores = jnp.where(allowed, scores, NEGATIVE)
-    highest = jnp.maximum(maxima, scores.max(-1))
-    weights = jnp.where(allowed, jnp.exp(scores - highest[..., None]), 0.0)
-    factor = jnp.exp(maxima - highest)
-    totals = totals * factor + weights.sum(-1)
-    summed = summed * factor[..., None] + jnp.einsum(
-        "hrk,khd->hrd",
-        weights.astype(jnp.bfloat16),
-        value_heads,
-        preferred_element_type=jnp.float32,
-    )
-    return (highest, totals, summed)
-
-
-def finish(fold_state):
-    maxima, totals, summed = fold_state
-    result = summed / totals[..., None]
-    return result.transpose(1, 0, 2).reshape(summed.shape[1], -1).astype(jnp.bfloat16)
-
-
-def key_block_rows():
-    return 512
+MESH = pl.DeviceIdType.MESH
+ROUNDS = 8
+SCALE = HEAD ** (-0.5) * 1.4426950408889634
+MASKED = -2e38
+EMPTY = -1e30
+
+
+def offset_of(r):
+    return (r + 1) // 2 * (2 * (r % 2) - 1)
+
+
+def landed(ref, sem):
+    pltpu.make_async_copy(ref, ref, sem).wait()
+
+
+def attention_kernel(
+    q_ref,
+    k_ref,
+    v_ref,
+    out_ref,
+    qbuf,
+    kvbuf,
+    acc,
+    maxima,
+    obuf,
+    abuf,
+    q_send,
+    kv_send,
+    own_send,
+    relay_send,
+    opp_send,
+    o_send,
+    q_recv,
+    kv_recv,
+    o_recv,
+):
+    b = lax.axis_index("blk")
+    z = lax.axis_index("wide")
+    sibling = b + 1 - 2 * lax.rem(b, 2)
+    up = lax.rem(b + 2, 8)
+    down = lax.rem(b + 6, 8)
+    across = lax.rem(b + 4, 8)
+
+    barrier = pltpu.get_barrier_semaphore()
+
+    @pl.loop(0, 64)
+    def _(i):
+        ib, iz = i // 8, lax.rem(i, 8)
+
+        @pl.when(i != b * 8 + z)
+        def _():
+            pl.semaphore_signal(
+                barrier, inc=1, device_id={"blk": ib, "wide": iz}, device_id_type=MESH
+            )
+
+    acc[...] = jnp.zeros_like(acc)
+    maxima[...] = jnp.full_like(maxima, EMPTY)
+    pl.semaphore_wait(barrier, 63)
+
+    def head_columns(h):
+        return pl.ds(pl.multiple_of(h * HEAD, HEAD), HEAD)
+
+    def kv_copies(r, h):
+        copies = []
+        for n, ref in enumerate((k_ref, v_ref)):
+            copies.append(
+                pltpu.make_async_remote_copy(
+                    src_ref=ref.at[:, head_columns(h)],
+                    dst_ref=kvbuf.at[r, n, b],
+                    send_sem=kv_send.at[r, n],
+                    recv_sem=kv_recv.at[r, b],
+                    device_id={"blk": b, "wide": h},
+                    device_id_type=MESH,
+                )
+            )
+        return copies
+
+    def q_copy(h):
+        return pltpu.make_async_remote_copy(
+            src_ref=q_ref.at[:, head_columns(h)],
+            dst_ref=qbuf.at[b],
+            send_sem=q_send.at[h],
+            recv_sem=q_recv.at[b],
+            device_id={"blk": z, "wide": h},
+            device_id_type=MESH,
+        )
+
+    def q_local():
+        return pltpu.make_async_copy(q_ref.at[:, head_columns(z)], qbuf.at[b], q_recv.at[b])
+
+    def is_self(h):
+        return jnp.logical_and(z == b, h == z)
+
+    @pl.when(z < FINE_HEADS)
+    def _():
+        for n, ref in enumerate((k_ref, v_ref)):
+            pltpu.make_async_copy(
+                ref.at[:, head_columns(z)], kvbuf.at[0, n, b], kv_recv.at[0, b]
+            ).start()
+
+    def send_round(r):
+        h = lax.rem(z - offset_of(r) + 8, 8)
+
+        @pl.when(h < FINE_HEADS)
+        def _():
+            for copy in kv_copies(r, h):
+                copy.start()
+
+    def wait_round(r):
+        h = lax.rem(z - offset_of(r) + 8, 8)
+
+        @pl.when(h < FINE_HEADS)
+        def _():
+            for copy in kv_copies(r, h):
+                copy.wait_send()
+
+    send_round(1)
+    send_round(2)
+
+    @pl.loop(0, FINE_HEADS)
+    def _(h):
+        @pl.when(is_self(h))
+        def _():
+            q_local().start()
+
+        @pl.when(jnp.logical_not(is_self(h)))
+        def _():
+            q_copy(h).start()
+
+    for r in range(3, ROUNDS):
+        send_round(r)
+
+    def piece(r, blk):
+        return kvbuf.at[r, :, blk]
+
+    def pass_on(src, sem, recv, blk):
+        return pltpu.make_async_remote_copy(
+            src_ref=src,
+            dst_ref=src,
+            send_sem=sem,
+            recv_sem=recv,
+            device_id={"blk": blk, "wide": z},
+            device_id_type=MESH,
+        )
+
+    def own_copies(r):
+        recv = kv_recv.at[r, b]
+        return [
+            pass_on(piece(r, b), own_send.at[r, n], recv, blk)
+            for n, blk in enumerate((up, down, sibling))
+        ]
+
+    def relay_copies(r):
+        return [
+            [
+                pass_on(kvbuf.at[r, 0, down], relay_send.at[r, 0], kv_recv.at[r, down], up),
+                pass_on(piece(r, down), relay_send.at[r, 1], kv_recv.at[r, down], sibling),
+            ],
+            [
+                pass_on(kvbuf.at[r, 1, up], relay_send.at[r, 2], kv_recv.at[r, up], down),
+                pass_on(piece(r, up), relay_send.at[r, 3], kv_recv.at[r, up], sibling),
+            ],
+        ]
+
+    def opp_copy(r):
+        return pass_on(piece(r, across), opp_send.at[r], kv_recv.at[r, across], sibling)
+
+    def compute(r):
+        source = lax.rem(z + offset_of(r) + 8, 8)
+        rows = lax.broadcasted_iota(jnp.int32, (HEAD, HEAD), 0)
+        cols = lax.broadcasted_iota(jnp.int32, (HEAD, HEAD), 1)
+        allowed = cols + (source - b) * HEAD <= rows
+        for n in range(8):
+            keys = kvbuf[r, 0, : n + 1].reshape((n + 1) * HEAD, HEAD)
+            values = kvbuf[r, 1, : n + 1].reshape((n + 1) * HEAD, HEAD)
+            scores = lax.dot_general(
+                qbuf[n], keys, (((1,), (1,)), ((), ())), preferred_element_type=jnp.float32
+            )
+            last = jnp.where(allowed, scores[:, n * HEAD :], MASKED)
+            if n:
+                scores = jnp.concatenate([scores[:, : n * HEAD], last], 1)
+            else:
+                scores = last
+            before = maxima[n]
+            highest = jnp.maximum(before, scores.max(-1, keepdims=True) * SCALE)
+            weights = jnp.exp2(scores * SCALE - jnp.concatenate([highest] * (n + 1), 1))
+            factor = jnp.exp2(before - highest)
+            extended = jnp.concatenate([values, jnp.ones_like(values)], 1)
+            summed = jnp.dot(
+                weights.astype(jnp.bfloat16), extended, preferred_element_type=jnp.float32
+            )
+            acc[n] = acc[n] * jnp.concatenate([factor, factor], 1) + summed
+            maxima[n] = highest
+
+    def o_copy(n):
+        return pltpu.make_async_remote_copy(
+            src_ref=obuf.at[n],
+            dst_ref=abuf.at[:, head_columns(z)],
+            send_sem=o_send.at[n],
+            recv_sem=o_recv,
+            device_id={"blk": n, "wide": b},
+            device_id_type=MESH,
+        )
+
+    def o_local(n):
+        return pltpu.make_async_copy(obuf.at[n], abuf.at[:, head_columns(z)], o_recv)
+
+    @pl.when(z < FINE_HEADS)
+    def _():
+        @pl.loop(0, ROUNDS + 3)
+        def _(i):
+            @pl.when(jnp.logical_and(i >= 1, i < ROUNDS + 1))
+            def _():
+                first, second = relay_copies(i - 1)
+                landed(piece(i - 1, down), kv_recv.at[i - 1, down])
+                for copy in first:
+                    copy.start()
+                landed(piece(i - 1, up), kv_recv.at[i - 1, up])
+                for copy in second:
+                    copy.start()
+
+            @pl.when(i < ROUNDS)
+            def _():
+                landed(piece(i, b), kv_recv.at[i, b])
+                for copy in own_copies(i):
+                    copy.start()
+
+            @pl.when(jnp.logical_and(i >= 2, i < ROUNDS + 2))
+            def _():
+                landed(piece(i - 2, across), kv_recv.at[i - 2, across])
+                opp_copy(i - 2).start()
+
+            @pl.when(i == 3)
+            def _():
+                for n in range(8):
+                    landed(qbuf.at[n], q_recv.at[n])
+
+            @pl.when(i >= 3)
+            def _():
+                for n in range(4):
+                    other = lax.rem(sibling + 2 * n, 8)
+                    landed(piece(i - 3, other), kv_recv.at[i - 3, other])
+                compute(i - 3)
+
+        for n in range(8):
+            total = acc[n]
+            obuf[n] = (total[:, :HEAD] / total[:, HEAD:]).astype(jnp.bfloat16)
+            here = jnp.logical_and(n == b, z == b)
+
+            @pl.when(here)
+            def _():
+                o_local(n).start()
+
+            @pl.when(jnp.logical_not(here))
+            def _():
+                o_copy(n).start()
+
+        @pl.loop(0, ROUNDS)
+        def _(r):
+            for copy in own_copies(r):
+                copy.wait_send()
+            for pair in relay_copies(r):
+                for copy in pair:
+                    copy.wait_send()
+            opp_copy(r).wait_send()
+
+        for n in range(8):
+
+            @pl.when(jnp.logical_not(jnp.logical_and(n == b, z == b)))
+            def _():
+                o_copy(n).wait_send()
+
+    for r in range(1, ROUNDS):
+        wait_round(r)
+
+    @pl.loop(0, FINE_HEADS)
+    def _(h):
+        @pl.when(jnp.logical_not(is_self(h)))
+        def _():
+            q_copy(h).wait_send()
+
+    landed(abuf, o_recv)
+    out_ref[...] = abuf[...]
+
+
+def attention(queries, key_rows, value_rows):
+    rows, width = queries.shape
+    vmem = pl.BlockSpec(memory_space=pltpu.VMEM)
+    dma = pltpu.SemaphoreType.DMA
+    return pl.pallas_call(
+        attention_kernel,
+        name="attention",
+        out_shape=jax.ShapeDtypeStruct((rows, width), jnp.bfloat16),
+        in_specs=[vmem] * 3,
+        out_specs=vmem,
+        scratch_shapes=[
+            pltpu.VMEM((8, rows, HEAD), jnp.bfloat16),
+            pltpu.VMEM((ROUNDS, 2, 8, rows, HEAD), jnp.bfloat16),
+            pltpu.VMEM((8, rows, 2 * HEAD), jnp.float32),
+            pltpu.VMEM((8, rows, HEAD), jnp.float32),
+            pltpu.VMEM((8, rows, HEAD), jnp.bfloat16),
+            pltpu.VMEM((rows, width), jnp.bfloat16),
+            dma((FINE_HEADS,)),
+            dma((ROUNDS, 2)),
+            dma((ROUNDS, 3)),
+            dma((ROUNDS, 4)),
+            dma((ROUNDS,)),
+            dma((8,)),
+            dma((8,)),
+            dma((ROUNDS, 8)),
+            dma,
+        ],
+        compiler_params=pltpu.CompilerParams(collective_id=0, has_side_effects=True),
+    )(queries, key_rows, value_rows)
 
 
 def local(
@@ -105,30 +377,7 @@
     reduce_weight,
     cotangent,
 ):
-    shard_rows = queries.shape[0]
-    self_index = lax.axis_index(("blk", "wide"))
-    query_position = self_index * shard_rows + jnp.arange(shard_rows, dtype=jnp.int32)
-    last_position = self_index * shard_rows + shard_rows - 1
-    key_piece, value_piece = side_by_side((key_rows, value_rows), ("blk", "wide"), 0, 1)
-    block_rows = key_block_rows()
-
-    def step(block_index, carry_state):
-        offset = block_index * block_rows
-        key_block = lax.dynamic_slice_in_dim(key_piece, offset, block_rows, 0)
-        value_block = lax.dynamic_slice_in_dim(value_piece, offset, block_rows, 0)
-        key_position = offset + jnp.arange(block_rows, dtype=jnp.int32)
-        return lax.cond(
-            offset <= last_position,
-            lambda current: attend(
-                current, queries, query_position, key_block, value_block, key_position
-            ),
-            lambda current: current,
-            carry_state,
-        )
-
-    attended = finish(
-        lax.fori_loop(0, key_piece.shape[0] // block_rows, step, empty_state(shard_rows))
-    )
+    attended = attention(queries, key_rows, value_rows)
     onehot = (token_ids[:, None] == jnp.arange(VOCAB, dtype=jnp.int32)[None, :]).astype(jnp.float32)
     stream = jnp.dot(
         onehot, embedding, precision=lax.Precision.HIGHEST, preferred_element_type=jnp.float32

time: 316 us -> 195 us (0.62)
  waiting for transfers between devices: 161 us -> 38.4 us
  Pallas kernels: 0 us -> 71.6 us
  starting transfers between devices: 72.1 us -> 33.7 us
  local copies, waits for them, and re-layouts: 37.9 us -> 12.8 us
    all_gather x2 -> x1, waiting for transfers between devices: 133 us -> 0.01 us  [side_by_side(): result = lax.all_gather(both, axis, axis=dim, tiled=True)]
    pallas_call x0 -> x1, Pallas kernels: none -> 71.6 us  [attention(): pl.pallas_call(attention_kernel, name='attention', out_shape=jax.ShapeDty...]
    all_to_all x1, starting transfers between devices: 42.3 us -> 5.1 us  [local(): lax.all_to_all(grad_wide, 'blk', split_axis=1, concat_axis=0, tiled=True)]
    split x1 -> x0, local copies, waits for them, and re-layouts: 17.3 us -> none  [side_by_side(): jnp.split(result, [sum(widths[:k]) for k in range(1, len(widths))], axis=...]
    all_to_all x2, waiting for transfers between devices: 16.3 us -> 24.6 us  [copy_for_each(): return lax.all_to_all(copies, axis, split_axis=0, concat_axis=0, tiled=True)]
    all_to_all x1, waiting for transfers between devices: 0.01 us -> 4.53 us  [local(): lax.all_to_all(grad_wide, 'blk', split_axis=1, concat_axis=0, tiled=True)]
    all_to_all x1, waiting for transfers between devices: 4.53 us -> 0.01 us  [local(): lax.all_to_all(normed, 'blk', split_axis=1, concat_axis=0, tiled=True)]
    dynamic_slice x3 -> x0, local copies, waits for them, and re-layouts: 4.45 us -> none  [step(): value_block = lax.dynamic_slice_in_dim(value_piece, offset, block_rows, 0)]
  transfers between devices with their start and end apart: 10 -> 9, of which waited for: 5 -> 4; matrix products, arithmetic and copies ran while one was open for 8% -> 11% of each run, Pallas kernels for 0% -> 0%
where the time goes in v1:
time: 195 us; the launch traced here: 194 us
  Pallas kernels  71.6 us (37%)
  waiting for transfers between devices  38.4 us (20%)
  starting transfers between devices  33.7 us (17%)
  matrix products  17 us (9%)
  between operations  14.3 us (7%)
  local copies, waits for them, and re-layouts  12.8 us (7%)
  other arithmetic  6.28 us (3%)
    pallas_call x1, Pallas kernels, attention(): pl.pallas_call(attention_kernel, name='attention', out_shape=jax.ShapeDty...  71.6 us
    all_to_all x2, waiting for transfers between devices, copy_for_each(): return lax.all_to_all(copies, axis, split_axis=0, concat_axis=0, tiled=True)  24.6 us
    ppermute x3, starting transfers between devices, from_behind(): return lax.ppermute(array, axis, pairs)  10.8 us
    all_to_all x1, waiting for transfers between devices, sum_at_owner(): lax.all_to_all(blocks, axis, split_axis=0, concat_axis=0, tiled=True)  9.24 us
    all_to_all x2, starting transfers between devices, copy_for_each(): return lax.all_to_all(copies, axis, split_axis=0, concat_axis=0, tiled=True)  8.93 us
    all_to_all x1, starting transfers between devices, local(): lax.all_to_all(grad_wide, 'blk', split_axis=1, concat_axis=0, tiled=True)  5.1 us
    all_to_all x1, starting transfers between devices, local(): lax.all_to_all(normed, 'blk', split_axis=1, concat_axis=0, tiled=True)  4.66 us
    all_to_all x1, waiting for transfers between devices, local(): lax.all_to_all(grad_wide, 'blk', split_axis=1, concat_axis=0, tiled=True)  4.53 us
  transfers between devices with their start and end apart: 9, of which 4 were waited for; matrix products, arithmetic and copies ran while one was open for 11% of the time, Pallas kernels for 0%

profile of v1, /device:TPU:1, one launch (start us, length us, event | category | flops | bytes accessed | tf_op | source)
XLA Modules:
  0.0 194.1 jit_solution(10970815780665376707)
XLA Ops:
  7.2 0.0 copy-start
  7.2 2.4 %fusion.25 = f32[128,1536]{1,0:T(8,128)} fusion(f32[6,1536]{1,0:T(8,128)} %param.10, s32[128]{0:T(128)} %param.9), kind=kOutput, calls=%fused_computation.44 | convolution fusion | flops 14156544 | bytes 823808 | tf_op jit(solution)/shard_map/dot_general | solution.py:382
  9.6 71.6 %attention.1 = bf16[128,768]{1,0:T(8,128)(2,1)} custom-call(bf16[128,768]{1,0:T(8,128)(2,1)} %q_ref.1, bf16[128,768]{1,0:T(8,128)(2,1)} %k_ref.1, bf16[128,768]{1,0:T(8,128)(2,1)} %v_ref.1), custom_call_target="tpu_custom_call" | custom-call | tf_op jit(solution)/shard_map/attention/pallas_call | solution.py:342
  81.2 0.0 copy-start.1
  81.2 1.8 convolution_add_fusion
  83.0 2.0 %collective-permute-start = (f32[1,1536]{1,0:T(1,128)S(1)}, f32[1,1536]{1,0:T(1,128)S(1)}, u32[]{:S(2)}, u32[]{:S(2)}) collective-permute-start(f32[1,1536]{1,0:T(1,128)S(1)} %slice.24), channel_id=1, source_target_pairs={{0,4},{4,8},{8,12},{12,16},{16,20},{20,24},{24,28},{28,32},{32,36}... | collective-permute-start | bytes 18440 | tf_op jit(solution)/shard_map/ppermute | solution.py:24
  85.0 0.3 fusion.13
  85.3 0.0 copy-start.4
  85.3 6.6 %collective-permute-start.2 = (f32[1,1536]{1,0:T(1,128)S(1)}, f32[1,1536]{1,0:T(1,128)S(1)}, u32[]{:S(2)}, u32[]{:S(2)}) collective-permute-start(f32[1,1536]{1,0:T(1,128)S(1)} %slice.29), channel_id=1, source_target_pairs={{4,0},{8,4},{12,8},{16,12},{20,16},{24,20},{28,24},{32,28},{36,32}... | collective-permute-start | bytes 18440 | tf_op jit(solution)/shard_map/ppermute | solution.py:24
  92.0 0.3 fusion.4
  92.3 0.6 copy-done.2
  92.9 0.8 broadcast_in_dim.4
  93.7 4.8 %all-to-all-start = ((bf16[8,16,1536]{2,1,0:T(8,128)(2,1)}), bf16[8,16,1536]{2,1,0:T(8,128)(2,1)S(1)}, u32[]{:S(2)}, u32[]{:S(2)}) async-start(bf16[8,16,1536]{2,1,0:T(8,128)(2,1)} %broadcast_in_dim.4), calls=%async_computation | async-start | bytes 786432 | tf_op jit(solution)/shard_map/all_to_all | solution.py:35
  98.5 1.2 fusion.15
  99.8 0.9 slice.28
  100.7 0.6 fusion.24
  101.4 12.2 %all-to-all-done = bf16[8,16,1536]{2,1,0:T(8,128)(2,1)S(1)} async-done(((bf16[8,16,1536]{2,1,0:T(8,128)(2,1)}), bf16[8,16,1536]{2,1,0:T(8,128)(2,1)S(1)}, u32[]{:S(2)}, u32[]{:S(2)}) %all-to-all-start) | async-done | bytes 393248 | tf_op jit(solution)/shard_map/all_to_all | solution.py:35
  113.6 1.6 broadcast_in_dim.5
  115.1 4.1 %all-to-all-start.3 = ((bf16[8,16,1536]{2,1,0:T(8,128)(2,1)}), bf16[8,16,1536]{2,1,0:T(8,128)(2,1)}, u32[]{:S(2)}, u32[]{:S(2)}) async-start(bf16[8,16,1536]{2,1,0:T(8,128)(2,1)} %broadcast_in_dim.5), calls=%async_computation.3 | async-start | bytes 786432 | tf_op jit(solution)/shard_map/all_to_all | solution.py:35
  119.2 0.0 all-gather.2.cloned.1.call-start
  119.3 0.1 multiply_reduce_fusion
  119.4 0.1 rsqrt.12
  119.5 0.2 fusion.8
  119.7 2.3 %fusion.33 = f32[128,384]{1,0:T(8,128)} fusion(bf16[128,1536]{1,0:T(8,128)(2,1)S(1)} %fusion.8, bf16[1536,384]{1,0:T(8,128)(2,1)} %param.15), kind=kOutput, calls=%fused_computation.55 | convolution fusion | flops 150994944 | bytes 1769472 | tf_op jit(solution)/shard_map/dot_general | solution.py:394
  122.0 12.4 %all-to-all-done.3 = bf16[8,16,1536]{2,1,0:T(8,128)(2,1)} async-done(((bf16[8,16,1536]{2,1,0:T(8,128)(2,1)}), bf16[8,16,1536]{2,1,0:T(8,128)(2,1)}, u32[]{:S(2)}, u32[]{:S(2)}) %all-to-all-start.3) | async-done | bytes 393248 | tf_op jit(solution)/shard_map/all_to_all | solution.py:35
  134.4 1.9 fusion.23
  136.3 0.0 copy-start.5
  136.3 0.6 copy-done.5
  136.9 0.7 pad_maximum_fusion
  137.6 0.0 all-gather.2.cloned.1.call-update
  137.7 2.4 %convolution_convert_fusion = bf16[128,1536]{1,0:T(8,128)(2,1)} fusion(bf16[128,384]{1,0:T(8,128)(2,1)} %copy-done.5, bf16[384,1536]{1,0:T(8,128)(2,1)} %param.16), kind=kOutput, calls=%fused_computation.1 | convolution fusion | flops 151191552 | bytes 1671168 | tf_op jit(solution)/shard_map/dot_general | solution.py:397
  140.1 4.1 %all-to-all-start.1 = ((bf16[8,16,1536]{2,1,0:T(8,128)(2,1)}), bf16[8,16,1536]{2,1,0:T(8,128)(2,1)}, u32[]{:S(2)}, u32[]{:S(2)}) async-start(bf16[8,16,1536]{2,1,0:T(8,128)(2,1)} %bitcast.66), calls=%async_computation.1 | async-start | bytes 786432 | tf_op jit(solution)/shard_map/all_to_all | solution.py:49
  144.2 1.3 reshape.83
  145.6 2.3 %multiply_convert_fusion = bf16[128,8,192]{2,1,0:T(8,128)(2,1)} fusion(f32[128,8,192]{2,1,0:T(8,128)} %reshape.83, f32[128]{0:T(128)S(1)} %rsqrt.12), kind=kLoop, calls=%fused_computation.2 | loop fusion | flops 393216 | bytes 1180160 | tf_op jit(solution)/shard_map/convert_element_type | solution.py:393
  147.9 2.2 %copy.14 = bf16[128,8,192]{0,2,1:T(8,128)(2,1)} copy(bf16[128,8,192]{2,1,0:T(8,128)(2,1)} %multiply_convert_fusion) | data formatting | bytes 786432 | tf_op jit(solution)/shard_map/convert_element_type | solution.py:393
  150.1 9.2 %all-to-all-done.1 = bf16[8,16,1536]{2,1,0:T(8,128)(2,1)} async-done(((bf16[8,16,1536]{2,1,0:T(8,128)(2,1)}), bf16[8,16,1536]{2,1,0:T(8,128)(2,1)}, u32[]{:S(2)}, u32[]{:S(2)}) %all-to-all-start.1) | async-done | bytes 393248 | tf_op jit(solution)/shard_map/all_to_all | solution.py:49
  159.3 4.7 %all-to-all-start.2 = ((bf16[128,8,192]{0,2,1:T(8,128)(2,1)}), bf16[128,8,192]{0,2,1:T(8,128)(2,1)}, u32[]{:S(2)}, u32[]{:S(2)}) async-start(bf16[128,8,192]{0,2,1:T(8,128)(2,1)} %copy.14), calls=%async_computation.2 | async-start | bytes 786432 | tf_op jit(solution)/shard_map/all_to_all | solution.py:422
  164.0 1.1 convert_reduce_fusion
  165.1 2.2 %collective-permute-start.1 = (f32[1,1536]{1,0:T(1,128)S(1)}, f32[1,1536]{1,0:T(1,128)S(1)}, u32[]{:S(2)}, u32[]{:S(2)}) collective-permute-start(f32[1,1536]{1,0:T(1,128)S(1)} %slice.26), channel_id=1, source_target_pairs={{0,4},{4,8},{8,12},{12,16},{16,20},{20,24},{24,28},{28,32},{32,36}... | collective-permute-start | bytes 18440 | tf_op jit(solution)/shard_map/ppermute | solution.py:24
  167.3 0.1 mul.114
  167.4 0.1 mul.120
  167.5 2.2 %all_to_all.41 = bf16[128,8,192]{2,1,0:T(8,128)(2,1)} reshape(bf16[8,16,1536]{2,1,0:T(8,128)(2,1)} %all-to-all-done.3) | data formatting | bytes 786432 | tf_op jit(solution)/shard_map/all_to_all | solution.py:423
  169.8 2.2 %copy.16 = bf16[128,8,192]{0,2,1:T(8,128)(2,1)} copy(bf16[128,8,192]{2,1,0:T(8,128)(2,1)} %all_to_all.41) | data formatting | bytes 786432 | tf_op jit(solution)/shard_map/all_to_all | solution.py:423
  172.0 5.1 %all-to-all-start.4 = ((bf16[128,8,192]{0,2,1:T(8,128)(2,1)}), bf16[128,8,192]{0,2,1:T(8,128)(2,1)}, u32[]{:S(2)}, u32[]{:S(2)}) async-start(bf16[128,8,192]{0,2,1:T(8,128)(2,1)} %copy.16), calls=%async_computation.4 | async-start | bytes 786432 | tf_op jit(solution)/shard_map/all_to_all | solution.py:423
  177.1 0.9 fusion.7
  178.0 2.3 %fusion.2 = f32[192,384]{1,0:T(8,128)} fusion(bf16[1024,768]{1,0:T(8,128)(2,1)} %all-gather.2.cloned.1.call-done, bf16[128,8,192]{0,2,1:T(8,128)(2,1)} %all-to-all-done.2), kind=kOutput, calls=%fused_computation.5 | convolution fusion | flops 150994944 | bytes 1474560 | tf_op jit(solution)/shard_map/gi,gj->ij/dot_general | solution.py:426
  180.4 4.5 %all-to-all-done.4 = bf16[128,8,192]{0,2,1:T(8,128)(2,1)} async-done(((bf16[128,8,192]{0,2,1:T(8,128)(2,1)}), bf16[128,8,192]{0,2,1:T(8,128)(2,1)}, u32[]{:S(2)}, u32[]{:S(2)}) %all-to-all-start.4) | async-done | bytes 393248 | tf_op jit(solution)/shard_map/all_to_all | solution.py:423
  184.9 2.3 %fusion = f32[384,192]{0,1:T(8,128)} fusion(bf16[1024,768]{1,0:T(8,128)(2,1)} %all-gather.2.cloned.1.call-done, bf16[128,8,192]{0,2,1:T(8,128)(2,1)} %all-to-all-done.4), kind=kOutput, calls=%fused_computation.3 | convolution fusion | flops 150994944 | bytes 1474560 | tf_op jit(solution)/shard_map/gi,gj->ij/dot_general | solution.py:427
  (23 shorter events, 0.1 us)
Async XLA Ops:
  7.2 74.0 %copy-start = (bf16[768,1536]{1,0:T(8,128)(2,1)S(1)}, bf16[768,1536]{1,0:T(8,128)(2,1)}, u32[]{:S(2)}) copy-start(bf16[768,1536]{1,0:T(8,128)(2,1)} %param.14) | copy-start | bytes 7077892
  81.2 3.8 %copy-start.1 = (bf16[128,1536]{1,0:T(8,128)(2,1)S(1)}, bf16[128,1536]{1,0:T(8,128)(2,1)}, u32[]{:S(2)}) copy-start(bf16[128,1536]{1,0:T(8,128)(2,1)} %param.17) | copy-start | bytes 1179652
  83.0 9.0 %collective-permute-start = (f32[1,1536]{1,0:T(1,128)S(1)}, f32[1,1536]{1,0:T(1,128)S(1)}, u32[]{:S(2)}, u32[]{:S(2)}) collective-permute-start(f32[1,1536]{1,0:T(1,128)S(1)} %slice.24), channel_id=1, source_target_pairs={{0,4},{4,8},{8,12},{12,16},{16,20},{20,24},{24,28},{28,32},{32,36}... | collective-permute-start | bytes 18440 | tf_op jit(solution)/shard_map/ppermute | solution.py:24
  85.3 6.7 %copy-start.4 = (f32[1,16,1536]{2,1,0:T(8,128)}, f32[1,16,1536]{2,1,0:T(8,128)S(1)}, u32[]{:S(2)}) copy-start(f32[1,16,1536]{2,1,0:T(8,128)S(1)} %copy.32) | copy-start | bytes 294916
  85.3 15.4 %collective-permute-start.2 = (f32[1,1536]{1,0:T(1,128)S(1)}, f32[1,1536]{1,0:T(1,128)S(1)}, u32[]{:S(2)}, u32[]{:S(2)}) collective-permute-start(f32[1,1536]{1,0:T(1,128)S(1)} %slice.29), channel_id=1, source_target_pairs={{4,0},{8,4},{12,8},{16,12},{20,16},{24,20},{28,24},{32,28},{36,32}... | collective-permute-start | bytes 18440 | tf_op jit(solution)/shard_map/ppermute | solution.py:24
  92.3 0.6 copy-start.2
  93.7 19.9 %all-to-all-start = ((bf16[8,16,1536]{2,1,0:T(8,128)(2,1)}), bf16[8,16,1536]{2,1,0:T(8,128)(2,1)S(1)}, u32[]{:S(2)}, u32[]{:S(2)}) async-start(bf16[8,16,1536]{2,1,0:T(8,128)(2,1)} %broadcast_in_dim.4), calls=%async_computation | async-start | bytes 786432 | tf_op jit(solution)/shard_map/all_to_all | solution.py:35
  115.1 19.2 %all-to-all-start.3 = ((bf16[8,16,1536]{2,1,0:T(8,128)(2,1)}), bf16[8,16,1536]{2,1,0:T(8,128)(2,1)}, u32[]{:S(2)}, u32[]{:S(2)}) async-start(bf16[8,16,1536]{2,1,0:T(8,128)(2,1)} %broadcast_in_dim.5), calls=%async_computation.3 | async-start | bytes 786432 | tf_op jit(solution)/shard_map/all_to_all | solution.py:35
  119.2 58.8 %all-gather.2.cloned.1.call-start = ((), (), s32[]{:S(2)}) async-start(), calls=%async_computation.5 | async-start | bytes 1769472 | tf_op jit(solution)/shard_map/all_gather | solution.py:17
  136.3 0.6 copy-start.5
  140.1 19.2 %all-to-all-start.1 = ((bf16[8,16,1536]{2,1,0:T(8,128)(2,1)}), bf16[8,16,1536]{2,1,0:T(8,128)(2,1)}, u32[]{:S(2)}, u32[]{:S(2)}) async-start(bf16[8,16,1536]{2,1,0:T(8,128)(2,1)} %bitcast.66), calls=%async_computation.1 | async-start | bytes 786432 | tf_op jit(solution)/shard_map/all_to_all | solution.py:49
  147.9 17.2 %copy-start.3 = (f32[16,1536]{1,0:T(8,128)S(1)}, f32[16,1536]{1,0:T(8,128)}, u32[]{:S(2)}) copy-start(f32[16,1536]{1,0:T(8,128)} %copy-done.2) | copy-start | bytes 294916
  159.3 12.7 %all-to-all-start.2 = ((bf16[128,8,192]{0,2,1:T(8,128)(2,1)}), bf16[128,8,192]{0,2,1:T(8,128)(2,1)}, u32[]{:S(2)}, u32[]{:S(2)}) async-start(bf16[128,8,192]{0,2,1:T(8,128)(2,1)} %copy.14), calls=%async_computation.2 | async-start | bytes 786432 | tf_op jit(solution)/shard_map/all_to_all | solution.py:422
  165.1 6.9 %collective-permute-start.1 = (f32[1,1536]{1,0:T(1,128)S(1)}, f32[1,1536]{1,0:T(1,128)S(1)}, u32[]{:S(2)}, u32[]{:S(2)}) collective-permute-start(f32[1,1536]{1,0:T(1,128)S(1)} %slice.26), channel_id=1, source_target_pairs={{0,4},{4,8},{8,12},{12,16},{16,20},{20,24},{24,28},{28,32},{32,36}... | collective-permute-start | bytes 18440 | tf_op jit(solution)/shard_map/ppermute | solution.py:24
  172.0 12.9 %all-to-all-start.4 = ((bf16[128,8,192]{0,2,1:T(8,128)(2,1)}), bf16[128,8,192]{0,2,1:T(8,128)(2,1)}, u32[]{:S(2)}, u32[]{:S(2)}) async-start(bf16[128,8,192]{0,2,1:T(8,128)(2,1)} %copy.16), calls=%async_computation.4 | async-start | bytes 786432 | tf_op jit(solution)/shard_map/all_to_all | solution.py:423
Sparse Core Ops, SparseCore 0:
  137.8 22.8 all-gather.1

commit v2 on v1

--- a/solution.py
+++ b/solution.py
@@ -8,50 +8,11 @@
 FINE_HEADS = 6
 HEAD = 128
 VOCAB = 6
-POOL = 8
-
-
-def side_by_side(arrays, axis, dim, along):
-    widths = [a.shape[along] for a in arrays]
-    both = jnp.concatenate(arrays, axis=along)
-    result = lax.all_gather(both, axis, axis=dim, tiled=True)
-    return tuple(jnp.split(result, [sum(widths[:k]) for k in range(1, len(widths))], axis=along))
-
-
-def from_behind(array, axis, by):
-    size = lax.axis_size(axis)
-    pairs = [(i, i + by) for i in range(size) if 0 <= i + by < size]
-    return lax.ppermute(array, axis, pairs)
-
-
-def in_order(blocks, dim):
-    shape = list(blocks.shape[1:])
-    shape[dim] *= blocks.shape[0]
-    return jnp.moveaxis(blocks, 0, dim).reshape(shape)
-
-
-def copy_for_each(array, axis):
-    copies = jnp.broadcast_to(array, (lax.axis_size(axis), *array.shape))
-    return lax.all_to_all(copies, axis, split_axis=0, concat_axis=0, tiled=True)
-
-
-def gather_directly(array, axis, dim):
-    return in_order(copy_for_each(array, axis), dim)
-
-
-def in_blocks(array, dim, size):
-    before, after = (array.shape[:dim], array.shape[dim + 1 :])
-    return jnp.moveaxis(array.reshape(*before, size, -1, *after), dim, 0)
-
-
-def sum_at_owner(array, axis, dim):
-    blocks = in_blocks(array, dim, lax.axis_size(axis))
-    arrived = lax.all_to_all(blocks, axis, split_axis=0, concat_axis=0, tiled=True)
-    return arrived.astype(jnp.float32).sum(axis=0)
 
 
 MESH = pl.DeviceIdType.MESH
 ROUNDS = 8
+RELAY, ACROSS, LAST = 2, 3, 4
 SCALE = HEAD ** (-0.5) * 1.4426950408889634
 MASKED = -2e38
 EMPTY = -1e30
@@ -93,21 +54,52 @@
     down = lax.rem(b + 6, 8)
     across = lax.rem(b + 4, 8)
 
+    home = lax.rem(b + 3 * z, 8)
+
+    def holder(wide, h):
+        return lax.rem(wide + 5 * h, 8)
+
     barrier = pltpu.get_barrier_semaphore()
 
-    @pl.loop(0, 64)
-    def _(i):
-        ib, iz = i // 8, lax.rem(i, 8)
-
-        @pl.when(i != b * 8 + z)
+    def greet(blk, wide):
+        pl.semaphore_signal(
+            barrier, inc=1, device_id={"blk": blk, "wide": wide}, device_id_type=MESH
+        )
+
+    holds_head = z < FINE_HEADS
+    diagonal = z == home
+
+    @pl.loop(1, 8)
+    def _(j):
+        greet(b, lax.rem(z + j, 8))
+
+    @pl.loop(0, FINE_HEADS)
+    def _(h):
+        @pl.when(jnp.logical_not(jnp.logical_and(diagonal, h == z)))
         def _():
-            pl.semaphore_signal(
-                barrier, inc=1, device_id={"blk": ib, "wide": iz}, device_id_type=MESH
-            )
+            greet(holder(z, h), h)
+
+    @pl.when(holds_head)
+    def _():
+        @pl.loop(0, 8)
+        def _(n):
+            @pl.when(jnp.logical_not(jnp.logical_and(diagonal, n == b)))
+            def _():
+                greet(n, home)
+
+        for blk in (up, down, sibling):
+            greet(blk, z)
 
     acc[...] = jnp.zeros_like(acc)
     maxima[...] = jnp.full_like(maxima, EMPTY)
-    pl.semaphore_wait(barrier, 63)
+
+    @pl.when(holds_head)
+    def _():
+        pl.semaphore_wait(barrier, 24 - 2 * diagonal.astype(jnp.int32))
+
+    @pl.when(jnp.logical_not(holds_head))
+    def _():
+        pl.semaphore_wait(barrier, 13)
 
     def head_columns(h):
         return pl.ds(pl.multiple_of(h * HEAD, HEAD), HEAD)
@@ -133,7 +125,7 @@
             dst_ref=qbuf.at[b],
             send_sem=q_send.at[h],
             recv_sem=q_recv.at[b],
-            device_id={"blk": z, "wide": h},
+            device_id={"blk": holder(z, h), "wide": h},
             device_id_type=MESH,
         )
 
@@ -141,7 +133,7 @@
         return pltpu.make_async_copy(q_ref.at[:, head_columns(z)], qbuf.at[b], q_recv.at[b])
 
     def is_self(h):
-        return jnp.logical_and(z == b, h == z)
+        return jnp.logical_and(z == home, h == z)
 
     @pl.when(z < FINE_HEADS)
     def _():
@@ -221,7 +213,7 @@
         source = lax.rem(z + offset_of(r) + 8, 8)
         rows = lax.broadcasted_iota(jnp.int32, (HEAD, HEAD), 0)
         cols = lax.broadcasted_iota(jnp.int32, (HEAD, HEAD), 1)
-        allowed = cols + (source - b) * HEAD <= rows
+        allowed = cols + (source - home) * HEAD <= rows
         for n in range(8):
             keys = kvbuf[r, 0, : n + 1].reshape((n + 1) * HEAD, HEAD)
             values = kvbuf[r, 1, : n + 1].reshape((n + 1) * HEAD, HEAD)
@@ -250,7 +242,7 @@
             dst_ref=abuf.at[:, head_columns(z)],
             send_sem=o_send.at[n],
             recv_sem=o_recv,
-            device_id={"blk": n, "wide": b},
+            device_id={"blk": n, "wide": home},
             device_id_type=MESH,
         )
 
@@ -259,17 +251,10 @@
 
     @pl.when(z < FINE_HEADS)
     def _():
-        @pl.loop(0, ROUNDS + 3)
+        @pl.loop(0, ROUNDS + LAST)
         def _(i):
-            @pl.when(jnp.logical_and(i >= 1, i < ROUNDS + 1))
-            def _():
-                first, second = relay_copies(i - 1)
-                landed(piece(i - 1, down), kv_recv.at[i - 1, down])
-                for copy in first:
-                    copy.start()
-                landed(piece(i - 1, up), kv_recv.at[i - 1, up])
-                for copy in second:
-                    copy.start()
+            def stage(late):
+                return jnp.logical_and(i >= late, i < ROUNDS + late)
 
             @pl.when(i < ROUNDS)
             def _():
@@ -277,27 +262,40 @@
                 for copy in own_copies(i):
                     copy.start()
 
-            @pl.when(jnp.logical_and(i >= 2, i < ROUNDS + 2))
-            def _():
-                landed(piece(i - 2, across), kv_recv.at[i - 2, across])
-                opp_copy(i - 2).start()
-
-            @pl.when(i == 3)
+            @pl.when(stage(RELAY))
+            def _():
+                r = i - RELAY
+                first, second = relay_copies(r)
+                landed(piece(r, down), kv_recv.at[r, down])
+                for copy in first:
+                    copy.start()
+                landed(piece(r, up), kv_recv.at[r, up])
+                for copy in second:
+                    copy.start()
+
+            @pl.when(stage(ACROSS))
+            def _():
+                r = i - ACROSS
+                landed(piece(r, across), kv_recv.at[r, across])
+                opp_copy(r).start()
+
+            @pl.when(i == LAST)
             def _():
                 for n in range(8):
                     landed(qbuf.at[n], q_recv.at[n])
 
-            @pl.when(i >= 3)
-            def _():
+            @pl.when(i >= LAST)
+            def _():
+                r = i - LAST
                 for n in range(4):
                     other = lax.rem(sibling + 2 * n, 8)
-                    landed(piece(i - 3, other), kv_recv.at[i - 3, other])
-                compute(i - 3)
+                    landed(piece(r, other), kv_recv.at[r, other])
+                compute(r)
 
         for n in range(8):
             total = acc[n]
             obuf[n] = (total[:, :HEAD] / total[:, HEAD:]).astype(jnp.bfloat16)
-            here = jnp.logical_and(n == b, z == b)
+            here = jnp.logical_and(n == b, z == home)
 
             @pl.when(here)
             def _():
@@ -318,7 +316,7 @@
 
         for n in range(8):
 
-            @pl.when(jnp.logical_not(jnp.logical_and(n == b, z == b)))
+            @pl.when(jnp.logical_not(jnp.logical_and(n == b, z == home)))
             def _():
                 o_copy(n).wait_send()
 
@@ -366,6 +364,398 @@
     )(queries, key_rows, value_rows)
 
 
+def gelu_parts(x):
+    root = 0.7978845608028654
+    inner = jnp.tanh(root * (x + 0.044715 * x * x * x))
+    slope = 0.5 * (1.0 + inner) + 0.5 * x * (1.0 - inner * inner) * root * (
+        1.0 + 3 * 0.044715 * x * x
+    )
+    return 0.5 * x * (1.0 + inner), slope
+
+
+def middle_kernel(
+    tok_ref,
+    emb_ref,
+    att_ref,
+    mixer_ref,
+    w1_ref,
+    w2_ref,
+    cot_ref,
+    restored_ref,
+    expand_ref,
+    reduce_ref,
+    sbuf,
+    lbuf,
+    mbuf,
+    row_out,
+    row_in,
+    pw,
+    gw,
+    nbuf,
+    pbuf,
+    rsb,
+    ab,
+    nwin,
+    gwin,
+    row_send,
+    row_recv,
+    pw_send,
+    gw_send,
+    rs_send,
+    ab_send,
+    sib_send,
+    nwin_send,
+    gwin_send,
+    pw_recv,
+    gw_recv,
+    rs_recv,
+    ab_recv,
+    nwin_recv,
+    gwin_recv,
+):
+    b = lax.axis_index("blk")
+    z = lax.axis_index("wide")
+    place = b * 8 + z
+    sibling = b + 1 - 2 * lax.rem(b, 2)
+    first, last = place == 0, place == 63
+    not_first, not_last = place > 0, place < 63
+    following = {"blk": lax.rem(b + (z + 1) // 8, 8), "wide": lax.rem(z + 1, 8)}
+    preceding = {"blk": lax.rem(b + 8 - (8 - z) // 8, 8), "wide": lax.rem(z + 7, 8)}
+
+    barrier = pltpu.get_barrier_semaphore()
+
+    def greet(where):
+        pl.semaphore_signal(barrier, inc=1, device_id=where, device_id_type=MESH)
+
+    @pl.loop(1, 8)
+    def _(j):
+        greet({"blk": b, "wide": lax.rem(z + j, 8)})
+        greet({"blk": lax.rem(b + j, 8), "wide": z})
+
+    @pl.when(not_last)
+    def _():
+        greet(following)
+
+    @pl.when(not_first)
+    def _():
+        greet(preceding)
+
+    def remote(src, dst, send, recv, where):
+        return pltpu.make_async_remote_copy(
+            src_ref=src,
+            dst_ref=dst,
+            send_sem=send,
+            recv_sem=recv,
+            device_id=where,
+            device_id_type=MESH,
+        )
+
+    eight = lax.broadcasted_iota(jnp.int32, (8, 1536), 0)
+
+    def at_row(n, row):
+        return jnp.where(eight == n, jnp.broadcast_to(row, (8, 1536)), 0.0)
+
+    def row_copy(n, where):
+        return remote(row_out.at[n], row_in.at[n], row_send.at[n], row_recv.at[n], where)
+
+    short = lax.broadcasted_iota(jnp.int32, (16, 128), 0)
+    inside = lax.broadcasted_iota(jnp.int32, (16, 128), 1) - 8 * short
+    own = jnp.logical_and(inside >= 0, inside < 8)
+    inside = inside.astype(jnp.float32)
+    after = jnp.where(own, (inside + 1.0) / 8, 0.0).astype(jnp.bfloat16)
+    before = jnp.where(own, (7.0 - inside) / 8, 0.0).astype(jnp.bfloat16)
+    cot = cot_ref[...]
+    later_part = jnp.dot(before, cot, preferred_element_type=jnp.float32)
+    lbuf[:16] = later_part
+    row_out[1] = later_part[:1]
+
+    kind = lax.broadcasted_iota(jnp.int32, (VOCAB, 128), 0)
+    onehot = (kind == tok_ref[...]).astype(jnp.float32)
+    stream = lax.dot_general(
+        onehot,
+        emb_ref[...],
+        (((0,), (0,)), ((), ())),
+        precision=lax.Precision.HIGHEST,
+        preferred_element_type=jnp.float32,
+    )
+    stream = stream + jnp.dot(att_ref[...], mixer_ref[...], preferred_element_type=jnp.float32)
+    sbuf[8:] = stream
+    row_out[0] = stream[127:]
+
+    pl.semaphore_wait(
+        barrier, 14 + not_first.astype(jnp.int32) + not_last.astype(jnp.int32)
+    )
+
+    @pl.when(not_last)
+    def _():
+        row_copy(0, following).start()
+
+    @pl.when(not_first)
+    def _():
+        row_copy(1, preceding).start()
+
+    own_part = jnp.dot(after, cot, preferred_element_type=jnp.float32)
+
+    @pl.when(first)
+    def _():
+        row_in[0] = jnp.zeros((1, 1536), jnp.float32)
+        row_in[2] = jnp.zeros((1, 1536), jnp.float32)
+
+    @pl.when(last)
+    def _():
+        row_in[1] = jnp.zeros((1, 1536), jnp.float32)
+
+    @pl.when(not_first)
+    def _():
+        landed(row_in.at[0], row_recv.at[0])
+
+    sbuf[:8] = at_row(7, row_in[0])
+    short = lax.broadcasted_iota(jnp.int32, (16, 136), 0)
+    inside = lax.broadcasted_iota(jnp.int32, (16, 136), 1) - 8 * short
+    pool = jnp.where(jnp.logical_and(inside >= 7, inside < 15), 0.125, 0.0)
+    pooled = jnp.dot(
+        pool, sbuf[...], precision=lax.Precision.HIGHEST, preferred_element_type=jnp.float32
+    ).astype(jnp.bfloat16)
+    mine = pl.ds(pl.multiple_of(z * 16, 16), 16)
+    pw[mine, :] = pooled
+
+    def wide_copy(buf, send, recv, j):
+        where = {"blk": b, "wide": lax.rem(z + j, 8)}
+        return remote(buf.at[mine], buf.at[mine], send.at[j - 1], recv, where)
+
+    @pl.loop(1, 8)
+    def _(j):
+        wide_copy(pw, pw_send, pw_recv, j).start()
+
+    @pl.when(not_last)
+    def _():
+        landed(row_in.at[1], row_recv.at[1])
+
+    lbuf[16:] = at_row(0, row_in[1])
+    middle_grad = (own_part + lbuf[1:17]).astype(jnp.bfloat16)
+    gw[mine, :] = middle_grad
+
+    @pl.loop(1, 8)
+    def _(j):
+        wide_copy(gw, gw_send, gw_recv, j).start()
+
+    landed(pw.at[pl.ds(0, 112)], pw_recv)
+    pooled_wide = pw[...].astype(jnp.float32)
+    scale = lax.rsqrt(jnp.mean(pooled_wide * pooled_wide, -1, keepdims=True) + 1e-06)
+    normed = (pooled_wide * scale).astype(jnp.bfloat16)
+    nbuf[...] = normed
+    expanded = jnp.dot(normed, w1_ref[...], preferred_element_type=jnp.float32)
+    activated, slope = gelu_parts(expanded)
+    activated = activated.astype(jnp.bfloat16)
+    ab[b, :, :384] = activated
+    pbuf[...] = jnp.dot(
+        activated, w2_ref[...], preferred_element_type=jnp.float32
+    ).astype(jnp.bfloat16)
+
+    def sum_copy(j):
+        to = lax.rem(z + j, 8)
+        return remote(
+            pbuf.at[pl.ds(pl.multiple_of(to * 16, 16), 16)],
+            rsb.at[j - 1],
+            rs_send.at[j - 1],
+            rs_recv,
+            {"blk": b, "wide": to},
+        )
+
+    @pl.loop(1, 8)
+    def _(j):
+        sum_copy(j).start()
+
+    landed(gw.at[pl.ds(0, 112)], gw_recv)
+    act_grad = lax.dot_general(
+        gw[...], w2_ref[...], (((1,), (1,)), ((), ())), preferred_element_type=jnp.float32
+    )
+    ab[b, :, 384:] = (act_grad * slope).astype(jnp.bfloat16)
+
+    def same_core(j):
+        return remote(
+            ab.at[b],
+            ab.at[b],
+            ab_send.at[j - 1],
+            ab_recv.at[b],
+            {"blk": lax.rem(b + 2 * j, 8), "wide": z},
+        )
+
+    def share(slot, n):
+        return remote(
+            ab.at[slot], ab.at[slot], sib_send.at[n], ab_recv.at[slot], {"blk": sibling, "wide": z}
+        )
+
+    def window(ref, to):
+        return ref.at[:, pl.ds(pl.multiple_of(to * 192 // 128 * 128, 128), 256)]
+
+    def window_copy(src, dst, send, recv, j):
+        to = lax.rem(b + j, 8)
+        return remote(
+            window(src, to), dst.at[b], send.at[j - 1], recv, {"blk": to, "wide": z}
+        )
+
+    @pl.loop(1, 4)
+    def _(j):
+        same_core(j).start()
+
+    share(b, 0).start()
+    kept = [
+        pltpu.make_async_copy(window(nbuf, b), nwin.at[b], nwin_send.at[7]),
+        pltpu.make_async_copy(window(gw, b), gwin.at[b], gwin_send.at[7]),
+    ]
+    for copy in kept:
+        copy.start()
+
+    @pl.loop(1, 8)
+    def _(j):
+        window_copy(nbuf, nwin, nwin_send, nwin_recv, j).start()
+
+    @pl.loop(1, 8)
+    def _(j):
+        window_copy(gw, gwin, gwin_send, gwin_recv, j).start()
+
+    landed(rsb, rs_recv)
+    middle = pw[mine, :].astype(jnp.float32) + pbuf[mine, :].astype(jnp.float32)
+    for n in range(7):
+        middle = middle + rsb[n].astype(jnp.float32)
+    mbuf[8:] = middle
+    row_out[2] = middle[15:]
+
+    @pl.when(not_last)
+    def _():
+        row_copy(2, following).start()
+
+    for j in range(1, 4):
+        slot = lax.rem(b + 2 * j, 8)
+        landed(ab.at[slot], ab_recv.at[slot])
+        share(slot, j).start()
+
+    @pl.when(not_first)
+    def _():
+        landed(row_in.at[2], row_recv.at[2])
+
+    mbuf[:8] = at_row(7, row_in[2])
+    steps = lax.broadcasted_iota(jnp.int32, (8, 1536), 0).astype(jnp.float32)
+    ahead, behind = (steps + 1.0) / 8, (7.0 - steps) / 8
+    for j in range(0, 16, 2):
+        rows = [
+            sbuf[8 * (n + 1) : 8 * (n + 2)]
+            + mbuf[8 + n : 9 + n] * ahead
+            + mbuf[7 + n : 8 + n] * behind
+            for n in (j, j + 1)
+        ]
+        restored_ref[8 * j : 8 * (j + 2)] = jnp.concatenate(rows, 0).astype(jnp.bfloat16)
+
+    for n in range(4):
+        slot = lax.rem(sibling + 2 * n, 8)
+        landed(ab.at[slot], ab_recv.at[slot])
+    landed(nwin.at[pl.ds(0, 7)], nwin_recv)
+    landed(gwin.at[pl.ds(0, 7)], gwin_recv)
+    for copy in kept:
+        copy.wait()
+    tokens = (((0,), (0,)), ((), ()))
+    both = ab[...].reshape(1024, 768)
+    expanded = lax.dot_general(
+        nwin[...].reshape(1024, 256), both[:, 384:], tokens, preferred_element_type=jnp.float32
+    )
+    odd = lax.rem(b, 2)
+    reduced = lax.dot_general(
+        both[:, :384], gwin[...].reshape(1024, 256), tokens, preferred_element_type=jnp.float32
+    )
+
+    @pl.when(odd == 0)
+    def _():
+        expand_ref[...] = expanded[:192]
+        reduce_ref[...] = reduced[:, :192]
+
+    @pl.when(odd == 1)
+    def _():
+        expand_ref[...] = expanded[64:]
+        reduce_ref[...] = reduced[:, 64:]
+
+    @pl.when(not_last)
+    def _():
+        row_copy(0, following).wait_send()
+        row_copy(2, following).wait_send()
+
+    @pl.when(not_first)
+    def _():
+        row_copy(1, preceding).wait_send()
+
+    @pl.loop(1, 8)
+    def _(j):
+        wide_copy(pw, pw_send, pw_recv, j).wait_send()
+        wide_copy(gw, gw_send, gw_recv, j).wait_send()
+        sum_copy(j).wait_send()
+        window_copy(nbuf, nwin, nwin_send, nwin_recv, j).wait_send()
+        window_copy(gw, gwin, gwin_send, gwin_recv, j).wait_send()
+
+    @pl.loop(1, 4)
+    def _(j):
+        same_core(j).wait_send()
+
+    share(b, 0).wait_send()
+    for j in range(1, 4):
+        share(lax.rem(b + 2 * j, 8), j).wait_send()
+
+
+def finish_step(token_ids, embedding, attended, head_mixer, expand_weight, reduce_weight, cotangent):
+    vmem = pl.BlockSpec(memory_space=pltpu.VMEM)
+    dma = pltpu.SemaphoreType.DMA
+    f32, bf16 = jnp.float32, jnp.bfloat16
+    return pl.pallas_call(
+        middle_kernel,
+        name="middle",
+        out_shape=(
+            jax.ShapeDtypeStruct((128, 1536), bf16),
+            jax.ShapeDtypeStruct((192, 384), f32),
+            jax.ShapeDtypeStruct((384, 192), f32),
+        ),
+        in_specs=[vmem] * 7,
+        out_specs=(vmem,) * 3,
+        scratch_shapes=[
+            pltpu.VMEM((136, 1536), f32),
+            pltpu.VMEM((24, 1536), f32),
+            pltpu.VMEM((24, 1536), f32),
+            pltpu.VMEM((3, 1, 1536), f32),
+            pltpu.VMEM((3, 1, 1536), f32),
+            pltpu.VMEM((128, 1536), bf16),
+            pltpu.VMEM((128, 1536), bf16),
+            pltpu.VMEM((128, 1536), bf16),
+            pltpu.VMEM((128, 1536), bf16),
+            pltpu.VMEM((7, 16, 1536), bf16),
+            pltpu.VMEM((8, 128, 768), bf16),
+            pltpu.VMEM((8, 128, 256), bf16),
+            pltpu.VMEM((8, 128, 256), bf16),
+            dma((3,)),
+            dma((3,)),
+            dma((7,)),
+            dma((7,)),
+            dma((7,)),
+            dma((3,)),
+            dma((4,)),
+            dma((8,)),
+            dma((8,)),
+            dma,
+            dma,
+            dma,
+            dma((8,)),
+            dma,
+            dma,
+        ],
+        compiler_params=pltpu.CompilerParams(collective_id=1, has_side_effects=True),
+    )(
+        token_ids.reshape(1, -1),
+        embedding,
+        attended,
+        head_mixer,
+        expand_weight,
+        reduce_weight,
+        cotangent,
+    )
+
+
 def local(
     token_ids,
     embedding,
@@ -378,54 +768,9 @@
     cotangent,
 ):
     attended = attention(queries, key_rows, value_rows)
-    onehot = (token_ids[:, None] == jnp.arange(VOCAB, dtype=jnp.int32)[None, :]).astype(jnp.float32)
-    stream = jnp.dot(
-        onehot, embedding, precision=lax.Precision.HIGHEST, preferred_element_type=jnp.float32
-    )
-    stream = stream + jnp.dot(attended, head_mixer, preferred_element_type=jnp.float32)
-    carried = from_behind(stream[-1:], ("blk", "wide"), 1)
-    shifted = jnp.concatenate([carried, stream[:-1]], 0)
-    pooled = shifted.reshape(-1, POOL, stream.shape[1]).mean(axis=1).astype(jnp.bfloat16)
-    pooled_wide = gather_directly(pooled, "wide", 0)
-    pooled_float = pooled_wide.astype(jnp.float32)
-    normed = (
-        pooled_float * lax.rsqrt(jnp.mean(pooled_float * pooled_float, -1, keepdims=True) + 1e-06)
-    ).astype(jnp.bfloat16)
-    expanded = jnp.dot(normed, expand_weight, preferred_element_type=jnp.float32)
-    activated = jax.nn.gelu(expanded).astype(jnp.bfloat16)
-    middle = pooled.astype(jnp.float32) + sum_at_owner(
-        jnp.dot(activated, reduce_weight, preferred_element_type=jnp.float32).astype(jnp.bfloat16),
-        "wide",
-        0,
-    )
-    earlier = from_behind(middle[-1:], ("blk", "wide"), 1)
-    before = jnp.concatenate([earlier, middle[:-1]], 0)
-    steps_index = jnp.arange(POOL, dtype=jnp.float32)
-    after_weights = (steps_index + 1.0) / POOL
-    before_weights = (POOL - 1.0 - steps_index) / POOL
-    upsampled = (
-        middle[:, None, :] * after_weights[None, :, None]
-        + before[:, None, :] * before_weights[None, :, None]
-    ).reshape(stream.shape)
-    restored = (stream + upsampled).astype(jnp.bfloat16)
-    grad_rows = cotangent.astype(jnp.float32).reshape(-1, POOL, stream.shape[1])
-    own_part = jnp.einsum("sid,i->sd", grad_rows, after_weights)
-    later_part = jnp.einsum("sid,i->sd", grad_rows, before_weights)
-    following = from_behind(later_part[:1], ("blk", "wide"), -1)
-    middle_grad = (own_part + jnp.concatenate([later_part[1:], following], 0)).astype(jnp.bfloat16)
-    grad_wide = gather_directly(middle_grad, "wide", 0)
-    act_grad = lax.dot_general(
-        grad_wide, reduce_weight, (((1,), (1,)), ((), ())), preferred_element_type=jnp.float32
-    )
-    pre_grad = jax.vjp(jax.nn.gelu, expanded)[1](act_grad)[0].astype(jnp.bfloat16)
-    normed_cols, grad_cols = (
-        lax.all_to_all(normed, "blk", split_axis=1, concat_axis=0, tiled=True),
-        lax.all_to_all(grad_wide, "blk", split_axis=1, concat_axis=0, tiled=True),
-    )
-    pre_all, act_all = side_by_side((pre_grad, activated), "blk", 0, 1)
-    expand_grad = jnp.einsum("gi,gj->ij", normed_cols, pre_all, preferred_element_type=jnp.float32)
-    reduce_grad = jnp.einsum("gi,gj->ij", act_all, grad_cols, preferred_element_type=jnp.float32)
-    return (restored, expand_grad, reduce_grad)
+    return finish_step(
+        token_ids, embedding, attended, head_mixer, expand_weight, reduce_weight, cotangent
+    )
 
 
 def solution(mesh):

time: 195 us -> 125 us (0.64)
  Pallas kernels: 71.6 us -> 119 us
  waiting for transfers between devices: 38.4 us -> 0 us
  starting transfers between devices: 33.7 us -> 0 us
  matrix products: 17 us -> 0 us
  between operations: 14.3 us -> 0.66 us
  local copies, waits for them, and re-layouts: 12.8 us -> 4.39 us
  other arithmetic: 6.28 us -> 0 us
    pallas_call x0 -> x1, Pallas kernels: none -> 54.6 us  [finish_step(): pl.pallas_call(middle_kernel, name='middle', out_shape=(jax.ShapeDtypeStr...]
    all_to_all x5 -> x0, waiting for transfers between devices: 38.3 us -> none  [the longest x2 24.6 us: copy_for_each(): return lax.all_to_all(copies, axis, split_axis=0, concat_axis=0, tiled=True)]
    all_to_all x5 -> x0, starting transfers between devices: 22.8 us -> none  [the longest x2 8.93 us: copy_for_each(): return lax.all_to_all(copies, axis, split_axis=0, concat_axis=0, tiled=True)]
    dot_general x9 -> x0, matrix products: 17 us -> none  [the longest x1 2.45 us: local(): jnp.dot(activated, reduce_weight, preferred_element_type=jnp.float32)]
    ppermute x3 -> x0, starting transfers between devices: 10.8 us -> none  [from_behind(): return lax.ppermute(array, axis, pairs)]
    pallas_call x1, Pallas kernels: 71.6 us -> 64.8 us  [attention(): pl.pallas_call(attention_kernel, name='attention', out_shape=jax.ShapeDty...]
    all_to_all x2 -> x0, local copies, waits for them, and re-layouts: 4.44 us -> none  [local(): lax.all_to_all(grad_wide, 'blk', split_axis=1, concat_axis=0, tiled=True)]
    convert_element_type x5 -> x0, other arithmetic: 4.04 us -> none  [the longest x2 2.46 us: local(): normed = (pooled_float * lax.rsqrt(jnp.mean(pooled_float * pooled_float,...]
  transfers between devices with their start and end apart: 9 -> 0, of which waited for: 4 -> 0; matrix products, arithmetic and copies ran while one was open for 11% -> 0% of each run, Pallas kernels for 0% -> 0%
where the time goes in v2:
time: 125 us; the launch traced here: 124 us
  Pallas kernels  119 us (95%)
  local copies, waits for them, and re-layouts  4.39 us (4%)
    pallas_call x1, Pallas kernels, attention(): pl.pallas_call(attention_kernel, name='attention', out_shape=jax.ShapeDty...  64.8 us
    pallas_call x1, Pallas kernels, finish_step(): pl.pallas_call(middle_kernel, name='middle', out_shape=(jax.ShapeDtypeStr...  54.6 us

profile of v2, /device:TPU:1, one launch (start us, length us, event | category | flops | bytes accessed | tf_op | source)
XLA Modules:
  0.0 124.4 jit_solution(15401443398926363744)
XLA Ops:
  0.6 64.8 %attention.1.att_ref = bf16[128,768]{1,0:T(8,128)(2,1)} custom-call(bf16[128,768]{1,0:T(8,128)(2,1)} %q_ref.1, bf16[128,768]{1,0:T(8,128)(2,1)} %k_ref.1, bf16[128,768]{1,0:T(8,128)(2,1)} %v_ref.1), custom_call_target="tpu_custom_call" | custom-call | tf_op jit(solution)/shard_map/attention/pallas_call | solution.py:340
  65.5 54.6 %middle.1 = (bf16[128,1536]{1,0:T(8,128)(2,1)}, f32[192,384]{1,0:T(8,128)}, f32[384,192]{1,0:T(8,128)}) custom-call(s32[1,128]{1,0:T(1,128)} %bitcast.1, f32[6,1536]{1,0:T(8,128)} %emb_ref.1, bf16[128,768]{1,0:T(8,128)(2,1)} %attention.1.att_ref, bf16[768,1536]{1,0:T(8,128)(2,1)} %mixer_ref.1, bf16[1536,384]{1,0:T(8,128)(2,1)} %w1_ref.1, ...), custom_call_target="tpu_custom_call" | custom-call | tf_op jit(solution)/shard_map/middle/pallas_call | solution.py:707
  120.0 0.0 copy-start
  120.1 1.9 %copy.12 = f32[384,192]{0,1:T(8,128)} copy(f32[384,192]{1,0:T(8,128)} %get-tuple-element.5) | data formatting | bytes 589824 | tf_op jit(solution)/shard_map/middle/pallas_call | solution.py:707
  122.0 1.8 %copy.15 = bf16[128,1536]{1,0:T(8,128)(2,1)} copy(bf16[128,1536]{1,0:T(8,128)(2,1)} %get-tuple-element.9) | data formatting | bytes 786432
  123.7 0.0 copy-done
  123.7 0.7 copy.16
Async XLA Ops:
  120.0 3.7 %copy-start = (f32[192,384]{1,0:T(8,128)S(1)}, f32[192,384]{1,0:T(8,128)}, u32[]{:S(2)}) copy-start(f32[192,384]{1,0:T(8,128)} %get-tuple-element.10) | copy-start | bytes 884740

commit v3 on v1

v3 whole, which is shorter than its diff:
```python
import jax
import jax.numpy as jnp
from jax import lax
from jax.experimental import pallas as pl
from jax.experimental.pallas import tpu as pltpu
from jax.sharding import PartitionSpec as P

FINE_HEADS = 6
HEAD = 128
VOCAB = 6


MESH = pl.DeviceIdType.MESH
ROUNDS = 8
RELAY, ACROSS, LAST = 2, 3, 4
LEAD = 3
SCALE = HEAD ** (-0.5) * 1.4426950408889634
MASKED = -2e38
EMPTY = -1e30


def offset_of(r):
    return (r + 1) // 2 * (2 * (r % 2) - 1)


def landed(ref, sem):
    pltpu.make_async_copy(ref, ref, sem).wait()


def gelu_parts(x):
    root = 0.7978845608028654
    inner = jnp.tanh(root * (x + 0.044715 * x * x * x))
    slope = 0.5 * (1.0 + inner) + 0.5 * x * (1.0 - inner * inner) * root * (
        1.0 + 3 * 0.044715 * x * x
    )
    return 0.5 * x * (1.0 + inner), slope


def step_kernel(
    tok_ref,
    emb_ref,
    q_ref,
    k_ref,
    v_ref,
    cot_ref,
    mixer_hbm,
    w1_hbm,
    w2_hbm,
    restored_ref,
    grads_ref,
    qbuf,
    kvbuf,
    acc,
    maxima,
    obuf,
    pobuf,
    abuf,
    pst,
    mixer_ref,
    w1_ref,
    w2_ref,
    lbuf,
    obuf16,
    mbuf,
    row_out,
    row_in,
    tok_in,
    cw,
    pw,
    gw,
    nbuf,
    pbuf,
    rsb,
    ab,
    nwin,
    gwin,
    sbuf,
    ready,
    w_sem,
    q_send,
    kv_send,
    own_send,
    relay_send,
    opp_send,
    o_send,
    po_send,
    px_send,
    q_recv,
    kv_recv,
    o_recv,
    po_recv,
    px_recv,
    row_send,
    row_recv,
    tok_send,
    tok_recv,
    cw_send,
    cw_recv,
    gw_send,
    rs_send,
    ab_send,
    sib_send,
    nwin_send,
    gwin_send,
    gw_recv,
    rs_recv,
    ab_recv,
    nwin_recv,
    gwin_recv,
):
    b = lax.axis_index("blk")
    z = lax.axis_index("wide")
    place = b * 8 + z
    sibling = b + 1 - 2 * lax.rem(b, 2)
    up = lax.rem(b + 2, 8)
    down = lax.rem(b + 6, 8)
    across = lax.rem(b + 4, 8)
    home = lax.rem(b + 3 * z, 8)
    holds_head = z < FINE_HEADS
    first, last = place == 0, place == 63
    not_first, not_last = place > 0, place < 63
    following = {"blk": lax.rem(b + (z + 1) // 8, 8), "wide": lax.rem(z + 1, 8)}
    preceding = {"blk": lax.rem(b + 8 - (8 - z) // 8, 8), "wide": lax.rem(z + 7, 8)}

    def holder(wide, h):
        return lax.rem(wide + 5 * h, 8)

    barrier = pltpu.get_barrier_semaphore()

    def greet(sem, where):
        pl.semaphore_signal(sem, inc=1, device_id=where, device_id_type=MESH)

    @pl.loop(1, 8)
    def _(j):
        greet(barrier, {"blk": b, "wide": lax.rem(z + j, 8)})
        greet(barrier, {"blk": lax.rem(b + j, 8), "wide": z})

    weights_in = [
        pltpu.make_async_copy(src, dst, w_sem.at[n])
        for n, (src, dst) in enumerate(
            ((mixer_hbm, mixer_ref), (w1_hbm, w1_ref), (w2_hbm, w2_ref))
        )
    ]
    for copy in weights_in:
        copy.start()

    def remote(src, dst, send, recv, where):
        return pltpu.make_async_remote_copy(
            src_ref=src,
            dst_ref=dst,
            send_sem=send,
            recv_sem=recv,
            device_id=where,
            device_id_type=MESH,
        )

    eight = lax.broadcasted_iota(jnp.int32, (8, 1536), 0)

    def at_row(n, row):
        return jnp.where(eight == n, jnp.broadcast_to(row, (8, 1536)), 0.0)

    def row_copy(n, where):
        return remote(row_out.at[n], row_in.at[n], row_send.at[n], row_recv.at[n], where)

    def tok_copy():
        return remote(tok_ref, tok_in, tok_send, tok_recv, following)

    short = lax.broadcasted_iota(jnp.int32, (16, 128), 0)
    inside = lax.broadcasted_iota(jnp.int32, (16, 128), 1) - 8 * short
    own = jnp.logical_and(inside >= 0, inside < 8)
    inside = inside.astype(jnp.float32)
    after = jnp.where(own, (inside + 1.0) / 8, 0.0).astype(jnp.bfloat16)
    before = jnp.where(own, (7.0 - inside) / 8, 0.0).astype(jnp.bfloat16)
    cot = cot_ref[...]
    later_part = jnp.dot(before, cot, preferred_element_type=jnp.float32)
    lbuf[:16] = later_part
    row_out[0] = later_part[:1]
    obuf16[...] = jnp.dot(after, cot, preferred_element_type=jnp.float32)
    acc[...] = jnp.zeros_like(acc)
    maxima[...] = jnp.full_like(maxima, EMPTY)

    @pl.when(last)
    def _():
        row_in[0] = jnp.zeros((1, 1536), jnp.float32)

    @pl.when(first)
    def _():
        row_in[1] = jnp.zeros((1, 1536), jnp.float32)
        tok_in[...] = jnp.full((1, 128), -1, jnp.int32)

    @pl.when(b == 0)
    def _():
        pst[256:] = jnp.zeros((16, 768), jnp.bfloat16)

    pl.semaphore_wait(barrier, 14)
    mine = pl.ds(pl.multiple_of(z * 16, 16), 16)

    def wide_copy(buf, send, recv, j):
        where = {"blk": b, "wide": lax.rem(z + j, 8)}
        return remote(buf.at[mine], buf.at[mine], send.at[j - 1], recv, where)

    def count_copy(j):
        where = {"blk": b, "wide": lax.rem(z + j, 8)}
        return remote(cw.at[z], cw.at[z], cw_send.at[j - 1], cw_recv, where)

    def send_grads():
        @pl.when(not_last)
        def _():
            landed(row_in.at[0], row_recv.at[0])

        lbuf[16:] = at_row(0, row_in[0])
        gw[mine, :] = (obuf16[...] + lbuf[1:17]).astype(jnp.bfloat16)

        @pl.loop(1, 8)
        def _(j):
            wide_copy(gw, gw_send, gw_recv, j).start()

        @pl.when(not_first)
        def _():
            landed(tok_in, tok_recv)

        lane = lax.broadcasted_iota(jnp.int32, (128, 128), 1)
        kind = lax.broadcasted_iota(jnp.int32, (128, 128), 0)
        shifted = jnp.where(
            lane == 0,
            pltpu.roll(jnp.broadcast_to(tok_in[...], (128, 128)), 1, 1),
            pltpu.roll(jnp.broadcast_to(tok_ref[...], (128, 128)), 1, 1),
        )
        short = lax.broadcasted_iota(jnp.int32, (16, 128), 0)
        inside = lax.broadcasted_iota(jnp.int32, (16, 128), 1) - 8 * short
        eighth = jnp.where(jnp.logical_and(inside >= 0, inside < 8), 0.125, 0.0)
        cw[z] = lax.dot_general(
            eighth.astype(jnp.bfloat16),
            jnp.where(kind == shifted, 1.0, 0.0).astype(jnp.bfloat16),
            (((1,), (1,)), ((), ())),
            preferred_element_type=jnp.float32,
        ).astype(jnp.bfloat16)

        @pl.loop(1, 8)
        def _(j):
            count_copy(j).start()

    def head_columns(h):
        return pl.ds(pl.multiple_of(h * HEAD, HEAD), HEAD)

    def kv_copies(r, h):
        copies = []
        for n, ref in enumerate((k_ref, v_ref)):
            copies.append(
                pltpu.make_async_remote_copy(
                    src_ref=ref.at[:, head_columns(h)],
                    dst_ref=kvbuf.at[r, n, b],
                    send_sem=kv_send.at[r, n],
                    recv_sem=kv_recv.at[r, b],
                    device_id={"blk": b, "wide": h},
                    device_id_type=MESH,
                )
            )
        return copies

    def q_copy(h):
        return pltpu.make_async_remote_copy(
            src_ref=q_ref.at[:, head_columns(h)],
            dst_ref=qbuf.at[b],
            send_sem=q_send.at[h],
            recv_sem=q_recv.at[b],
            device_id={"blk": holder(z, h), "wide": h},
            device_id_type=MESH,
        )

    def q_local():
        return pltpu.make_async_copy(q_ref.at[:, head_columns(z)], qbuf.at[b], q_recv.at[b])

    def is_self(h):
        return jnp.logical_and(z == home, h == z)

    @pl.when(z < FINE_HEADS)
    def _():
        for n, ref in enumerate((k_ref, v_ref)):
            pltpu.make_async_copy(
                ref.at[:, head_columns(z)], kvbuf.at[0, n, b], kv_recv.at[0, b]
            ).start()

    def send_round(r):
        h = lax.rem(z - offset_of(r) + 8, 8)

        @pl.when(h < FINE_HEADS)
        def _():
            for copy in kv_copies(r, h):
                copy.start()

    def wait_round(r):
        h = lax.rem(z - offset_of(r) + 8, 8)

        @pl.when(h < FINE_HEADS)
        def _():
            for copy in kv_copies(r, h):
                copy.wait_send()

    for r in range(1, LEAD + 1):
        send_round(r)

    def send_queries():
        @pl.loop(0, FINE_HEADS)
        def _(h):
            @pl.when(is_self(h))
            def _():
                q_local().start()

            @pl.when(jnp.logical_not(is_self(h)))
            def _():
                q_copy(h).start()

    @pl.loop(1, 8)
    def _(j):
        greet(ready, {"blk": lax.rem(b + j, 8), "wide": z})

    pl.semaphore_wait(ready, 7)
    send_queries()

    @pl.when(not_last)
    def _():
        tok_copy().start()

    @pl.when(not_first)
    def _():
        row_copy(0, preceding).start()

    @pl.when(jnp.logical_not(holds_head))
    def _():
        @pl.loop(1, ROUNDS)
        def _(r):
            wait_round(r)

            @pl.when(r < ROUNDS - LEAD)
            def _():
                send_round(r + LEAD)

        send_grads()

    def piece(r, blk):
        return kvbuf.at[r, :, blk]

    def pass_on(src, sem, recv, blk):
        return pltpu.make_async_remote_copy(
            src_ref=src,
            dst_ref=src,
            send_sem=sem,
            recv_sem=recv,
            device_id={"blk": blk, "wide": z},
            device_id_type=MESH,
        )

    def own_copies(r):
        recv = kv_recv.at[r, b]
        return [
            pass_on(piece(r, b), own_send.at[r, n], recv, blk)
            for n, blk in enumerate((up, down, sibling))
        ]

    def relay_copies(r):
        return [
            [
                pass_on(kvbuf.at[r, 0, down], relay_send.at[r, 0], kv_recv.at[r, down], up),
                pass_on(piece(r, down), relay_send.at[r, 1], kv_recv.at[r, down], sibling),
            ],
            [
                pass_on(kvbuf.at[r, 1, up], relay_send.at[r, 2], kv_recv.at[r, up], down),
                pass_on(piece(r, up), relay_send.at[r, 3], kv_recv.at[r, up], sibling),
            ],
        ]

    def opp_copy(r):
        return pass_on(piece(r, across), opp_send.at[r], kv_recv.at[r, across], sibling)

    def compute(r):
        source = lax.rem(z + offset_of(r) + 8, 8)
        rows = lax.broadcasted_iota(jnp.int32, (HEAD, HEAD), 0)
        cols = lax.broadcasted_iota(jnp.int32, (HEAD, HEAD), 1)
        allowed = cols + (source - home) * HEAD <= rows
        for n in range(8):
            keys = kvbuf[r, 0, : n + 1].reshape((n + 1) * HEAD, HEAD)
            values = kvbuf[r, 1, : n + 1].reshape((n + 1) * HEAD, HEAD)
            scores = lax.dot_general(
                qbuf[n], keys, (((1,), (1,)), ((), ())), preferred_element_type=jnp.float32
            )
            last = jnp.where(allowed, scores[:, n * HEAD :], MASKED)
            if n:
                scores = jnp.concatenate([scores[:, : n * HEAD], last], 1)
            else:
                scores = last
            before = maxima[n]
            highest = jnp.maximum(before, scores.max(-1, keepdims=True) * SCALE)
            weights = jnp.exp2(scores * SCALE - jnp.concatenate([highest] * (n + 1), 1))
            factor = jnp.exp2(before - highest)
            extended = jnp.concatenate([values, jnp.ones_like(values)], 1)
            summed = jnp.dot(
                weights.astype(jnp.bfloat16), extended, preferred_element_type=jnp.float32
            )
            acc[n] = acc[n] * jnp.concatenate([factor, factor], 1) + summed
            maxima[n] = highest

    def o_copy(n):
        return pltpu.make_async_remote_copy(
            src_ref=obuf.at[n],
            dst_ref=abuf.at[:, head_columns(z)],
            send_sem=o_send.at[n],
            recv_sem=o_recv,
            device_id={"blk": n, "wide": home},
            device_id_type=MESH,
        )

    def o_local(n):
        return pltpu.make_async_copy(obuf.at[n], abuf.at[:, head_columns(z)], o_recv)

    def pool_target():
        return pst.at[pl.ds(pl.multiple_of(home * 32, 32), 32), head_columns(z)]

    def pool_copy(n, w):
        return remote(
            pobuf.at[n], pool_target(), po_send.at[n, w], po_recv, {"blk": n, "wide": w}
        )

    def pool_local(n):
        return pltpu.make_async_copy(pobuf.at[n], pool_target(), po_recv)

    def edge_copy(n, w):
        return remote(
            pobuf.at[n, pl.ds(16, 16)],
            pst.at[pl.ds(256, 16), head_columns(z)],
            px_send.at[n, w],
            px_recv,
            {"blk": n + 1, "wide": w},
        )

    def edge_local(n):
        return pltpu.make_async_copy(
            pobuf.at[n, pl.ds(16, 16)], pst.at[pl.ds(256, 16), head_columns(z)], px_recv
        )

    def is_next(n, w):
        return jnp.logical_and(n + 1 == b, w == z)

    @pl.when(z < FINE_HEADS)
    def _():
        @pl.loop(0, ROUNDS + LAST)
        def _(i):
            def stage(late):
                return jnp.logical_and(i >= late, i < ROUNDS + late)

            @pl.when(i < ROUNDS)
            def _():
                landed(piece(i, b), kv_recv.at[i, b])

                @pl.when(jnp.logical_and(i > 0, i < ROUNDS - LEAD))
                def _():
                    send_round(i + LEAD)

                for copy in own_copies(i):
                    copy.start()

            @pl.when(stage(RELAY))
            def _():
                r = i - RELAY
                first, second = relay_copies(r)
                landed(piece(r, down), kv_recv.at[r, down])
                for copy in first:
                    copy.start()
                landed(piece(r, up), kv_recv.at[r, up])
                for copy in second:
                    copy.start()

            @pl.when(stage(ACROSS))
            def _():
                r = i - ACROSS
                landed(piece(r, across), kv_recv.at[r, across])
                opp_copy(r).start()

            @pl.when(i == LAST)
            def _():
                send_grads()
                for n in range(8):
                    landed(qbuf.at[n], q_recv.at[n])

            @pl.when(i >= LAST)
            def _():
                r = i - LAST
                for n in range(4):
                    other = lax.rem(sibling + 2 * n, 8)
                    landed(piece(r, other), kv_recv.at[r, other])
                compute(r)

        short = lax.broadcasted_iota(jnp.int32, (32, HEAD), 0)
        inside = lax.broadcasted_iota(jnp.int32, (32, HEAD), 1) - 8 * short
        taken = jnp.where(
            short < 16,
            jnp.logical_and(inside >= -1, inside < 7).astype(jnp.int32),
            jnp.logical_and(short == 16, inside == -1).astype(jnp.int32),
        )
        pool = jnp.where(taken == 1, 0.125, 0.0).astype(jnp.bfloat16)
        for n in range(8):
            total = acc[n]
            out = (total[:, :HEAD] / total[:, HEAD:]).astype(jnp.bfloat16)
            obuf[n] = out
            pobuf[n] = jnp.dot(pool, out, preferred_element_type=jnp.float32).astype(jnp.bfloat16)

            @pl.loop(0, 8)
            def _(w):
                at_self = jnp.logical_and(n == b, w == z)

                @pl.when(at_self)
                def _():
                    pool_local(n).start()

                @pl.when(jnp.logical_not(at_self))
                def _():
                    pool_copy(n, w).start()

                if n < 7:
                    crosses = home == 7

                    @pl.when(jnp.logical_and(crosses, is_next(n, w)))
                    def _():
                        edge_local(n).start()

                    @pl.when(jnp.logical_and(crosses, jnp.logical_not(is_next(n, w))))
                    def _():
                        edge_copy(n, w).start()

        for n in range(8):
            here = jnp.logical_and(n == b, z == home)

            @pl.when(here)
            def _():
                o_local(n).start()

            @pl.when(jnp.logical_not(here))
            def _():
                o_copy(n).start()

    landed(gw.at[pl.ds(0, 112)], gw_recv)
    def same_core(j):
        return remote(
            ab.at[b],
            ab.at[b],
            ab_send.at[j - 1],
            ab_recv.at[b],
            {"blk": lax.rem(b + 2 * j, 8), "wide": z},
        )

    def share(slot, n):
        return remote(
            ab.at[slot], ab.at[slot], sib_send.at[n], ab_recv.at[slot], {"blk": sibling, "wide": z}
        )

    def window(ref, to):
        return ref.at[:, pl.ds(pl.multiple_of(to * 192 // 128 * 128, 128), 256)]

    def window_copy(src, dst, send, recv, j):
        to = lax.rem(b + j, 8)
        return remote(
            window(src, to), dst.at[b], send.at[j - 1], recv, {"blk": to, "wide": z}
        )

    kept = [
        pltpu.make_async_copy(window(nbuf, b), nwin.at[b], nwin_send.at[7]),
        pltpu.make_async_copy(window(gw, b), gwin.at[b], gwin_send.at[7]),
    ]
    kept[1].start()

    @pl.loop(1, 8)
    def _(j):
        window_copy(gw, gwin, gwin_send, gwin_recv, j).start()

    for copy in weights_in:
        copy.wait()
    act_grad = lax.dot_general(
        gw[...], w2_ref[...], (((1,), (1,)), ((), ())), preferred_element_type=jnp.float32
    )

    landed(cw.at[pl.ds(0, 7)], cw_recv)
    counts = cw[...].reshape(128, 128)[:, :VOCAB].astype(jnp.float32)
    embedded = jnp.dot(
        counts,
        emb_ref[...],
        precision=lax.Precision.HIGHEST,
        preferred_element_type=jnp.float32,
    )
    row = lax.broadcasted_iota(jnp.int32, (128, 272), 0)
    col = lax.broadcasted_iota(jnp.int32, (128, 272), 1)
    group = lax.shift_right_logical(row, 4)
    within = jnp.bitwise_and(row, 15)
    edge = jnp.where(group == 0, 256, 32 * group - 16)
    picked = jnp.logical_or(
        col == 32 * group + within, jnp.logical_and(within == 0, col == edge)
    )
    picked = jnp.where(picked, 1.0, 0.0).astype(jnp.bfloat16)

    @pl.when(b > 0)
    def _():
        landed(pst.at[pl.ds(256, 16)], px_recv)

    landed(pst.at[pl.ds(0, 256)], po_recv)
    gathered = jnp.dot(picked, pst[...], preferred_element_type=jnp.float32).astype(jnp.bfloat16)
    pooled = embedded + jnp.dot(gathered, mixer_ref[...], preferred_element_type=jnp.float32)
    pooled = pooled.astype(jnp.bfloat16)
    pw[...] = pooled
    pooled_wide = pooled.astype(jnp.float32)
    scale = lax.rsqrt(jnp.mean(pooled_wide * pooled_wide, -1, keepdims=True) + 1e-06)
    normed = (pooled_wide * scale).astype(jnp.bfloat16)
    nbuf[...] = normed
    expanded = jnp.dot(normed, w1_ref[...], preferred_element_type=jnp.float32)
    activated, slope = gelu_parts(expanded)
    activated = activated.astype(jnp.bfloat16)
    pbuf[...] = jnp.dot(
        activated, w2_ref[...], preferred_element_type=jnp.float32
    ).astype(jnp.bfloat16)

    def sum_copy(j):
        to = lax.rem(z + j, 8)
        return remote(
            pbuf.at[pl.ds(pl.multiple_of(to * 16, 16), 16)],
            rsb.at[j - 1],
            rs_send.at[j - 1],
            rs_recv,
            {"blk": b, "wide": to},
        )

    @pl.loop(1, 8)
    def _(j):
        sum_copy(j).start()

    ab[b, :, :384] = activated
    ab[b, :, 384:] = (act_grad * slope).astype(jnp.bfloat16)

    @pl.loop(1, 4)
    def _(j):
        same_core(j).start()

    share(b, 0).start()
    kept[0].start()

    @pl.loop(1, 8)
    def _(j):
        window_copy(nbuf, nwin, nwin_send, nwin_recv, j).start()

    kind = lax.broadcasted_iota(jnp.int32, (VOCAB, 128), 0)
    onehot = (kind == tok_ref[...]).astype(jnp.float32)
    stream = lax.dot_general(
        onehot,
        emb_ref[...],
        (((0,), (0,)), ((), ())),
        precision=lax.Precision.HIGHEST,
        preferred_element_type=jnp.float32,
    )
    landed(abuf, o_recv)
    sbuf[...] = stream + jnp.dot(
        abuf[...], mixer_ref[...], preferred_element_type=jnp.float32
    )

    landed(rsb, rs_recv)
    middle = pw[mine, :].astype(jnp.float32) + pbuf[mine, :].astype(jnp.float32)
    for n in range(7):
        middle = middle + rsb[n].astype(jnp.float32)
    mbuf[8:] = middle
    row_out[1] = middle[15:]

    @pl.when(not_last)
    def _():
        row_copy(1, following).start()

    for j in range(1, 4):
        slot = lax.rem(b + 2 * j, 8)
        landed(ab.at[slot], ab_recv.at[slot])
        share(slot, j).start()

    @pl.when(not_first)
    def _():
        landed(row_in.at[1], row_recv.at[1])

    mbuf[:8] = at_row(7, row_in[1])
    steps = lax.broadcasted_iota(jnp.int32, (8, 1536), 0).astype(jnp.float32)
    ahead, behind = (steps + 1.0) / 8, (7.0 - steps) / 8
    for j in range(0, 16, 2):
        rows = [
            sbuf[8 * n : 8 * (n + 1)]
            + mbuf[8 + n : 9 + n] * ahead
            + mbuf[7 + n : 8 + n] * behind
            for n in (j, j + 1)
        ]
        restored_ref[8 * j : 8 * (j + 2)] = jnp.concatenate(rows, 0).astype(jnp.bfloat16)

    for n in range(4):
        slot = lax.rem(sibling + 2 * n, 8)
        landed(ab.at[slot], ab_recv.at[slot])
    landed(nwin.at[pl.ds(0, 7)], nwin_recv)
    landed(gwin.at[pl.ds(0, 7)], gwin_recv)
    for copy in kept:
        copy.wait()
    tokens = (((0,), (0,)), ((), ()))
    both = ab[...].reshape(1024, 768)
    expanded = lax.dot_general(
        nwin[...].reshape(1024, 256), both[:, 384:], tokens, preferred_element_type=jnp.float32
    )
    odd = lax.rem(b, 2)
    reduced = lax.dot_general(
        gwin[...].reshape(1024, 256), both[:, :384], tokens, preferred_element_type=jnp.float32
    )

    @pl.when(odd == 0)
    def _():
        grads_ref[0] = expanded[:192]
        grads_ref[1] = reduced[:192]

    @pl.when(odd == 1)
    def _():
        grads_ref[0] = expanded[64:]
        grads_ref[1] = reduced[64:]

    @pl.when(holds_head)
    def _():
        @pl.loop(0, ROUNDS)
        def _(r):
            for copy in own_copies(r):
                copy.wait_send()
            for pair in relay_copies(r):
                for copy in pair:
                    copy.wait_send()
            opp_copy(r).wait_send()

        @pl.loop(1, ROUNDS)
        def _(r):
            wait_round(r)

        @pl.loop(0, 8)
        def _(n):
            @pl.when(jnp.logical_not(jnp.logical_and(n == b, z == home)))
            def _():
                o_copy(n).wait_send()

            @pl.loop(0, 8)
            def _(w):
                @pl.when(jnp.logical_not(jnp.logical_and(n == b, w == z)))
                def _():
                    pool_copy(n, w).wait_send()

                @pl.when(
                    jnp.logical_and(
                        jnp.logical_and(home == 7, n < 7), jnp.logical_not(is_next(n, w))
                    )
                )
                def _():
                    edge_copy(n, w).wait_send()

    @pl.loop(0, FINE_HEADS)
    def _(h):
        @pl.when(jnp.logical_not(is_self(h)))
        def _():
            q_copy(h).wait_send()

    @pl.when(not_last)
    def _():
        row_copy(1, following).wait_send()
        tok_copy().wait_send()

    @pl.when(not_first)
    def _():
        row_copy(0, preceding).wait_send()

    @pl.loop(1, 8)
    def _(j):
        count_copy(j).wait_send()
        wide_copy(gw, gw_send, gw_recv, j).wait_send()
        sum_copy(j).wait_send()
        window_copy(nbuf, nwin, nwin_send, nwin_recv, j).wait_send()
        window_copy(gw, gwin, gwin_send, gwin_recv, j).wait_send()

    @pl.loop(1, 4)
    def _(j):
        same_core(j).wait_send()

    share(b, 0).wait_send()
    for j in range(1, 4):
        share(lax.rem(b + 2 * j, 8), j).wait_send()


def whole_step(*arrays):
    rows = 128
    vmem = pl.BlockSpec(memory_space=pltpu.VMEM)
    hbm = pl.BlockSpec(memory_space=pl.ANY)
    dma = pltpu.SemaphoreType.DMA
    f32, bf16 = jnp.float32, jnp.bfloat16
    return pl.pallas_call(
        step_kernel,
        name="step",
        out_shape=(
            jax.ShapeDtypeStruct((rows, 1536), bf16),
            jax.ShapeDtypeStruct((2, 192, 384), f32),
        ),
        in_specs=[vmem] * 6 + [hbm] * 3,
        out_specs=(vmem, vmem),
        scratch_shapes=[
            pltpu.VMEM((8, rows, HEAD), bf16),
            pltpu.VMEM((ROUNDS, 2, 8, rows, HEAD), bf16),
            pltpu.VMEM((8, rows, 2 * HEAD), f32),
            pltpu.VMEM((8, rows, HEAD), f32),
            pltpu.VMEM((8, rows, HEAD), bf16),
            pltpu.VMEM((8, 32, HEAD), bf16),
            pltpu.VMEM((rows, 768), bf16),
            pltpu.VMEM((272, 768), bf16),
            pltpu.VMEM((768, 1536), bf16),
            pltpu.VMEM((1536, 384), bf16),
            pltpu.VMEM((384, 1536), bf16),
            pltpu.VMEM((24, 1536), f32),
            pltpu.VMEM((16, 1536), f32),
            pltpu.VMEM((24, 1536), f32),
            pltpu.VMEM((2, 1, 1536), f32),
            pltpu.VMEM((2, 1, 1536), f32),
            pltpu.VMEM((1, 128), jnp.int32),
            pltpu.VMEM((8, 16, 128), bf16),
            pltpu.VMEM((128, 1536), bf16),
            pltpu.VMEM((128, 1536), bf16),
            pltpu.VMEM((128, 1536), bf16),
            pltpu.VMEM((128, 1536), bf16),
            pltpu.VMEM((7, 16, 1536), bf16),
            pltpu.VMEM((8, 128, 768), bf16),
            pltpu.VMEM((8, 128, 256), bf16),
            pltpu.VMEM((8, 128, 256), bf16),
            pltpu.VMEM((128, 1536), f32),
            pltpu.SemaphoreType.REGULAR,
            dma((3,)),
            dma((FINE_HEADS,)),
            dma((ROUNDS, 2)),
            dma((ROUNDS, 3)),
            dma((ROUNDS, 4)),
            dma((ROUNDS,)),
            dma((8,)),
            dma((8, 8)),
            dma((8, 8)),
            dma((8,)),
            dma((ROUNDS, 8)),
            dma,
            dma,
            dma,
            dma((2,)),
            dma((2,)),
            dma,
            dma,
            dma((7,)),
            dma,
            dma((7,)),
            dma((7,)),
            dma((3,)),
            dma((4,)),
            dma((8,)),
            dma((8,)),
            dma,
            dma,
            dma((8,)),
            dma,
            dma,
        ],
        compiler_params=pltpu.CompilerParams(collective_id=0, has_side_effects=True),
    )(*arrays)


def local(
    token_ids,
    embedding,
    queries,
    key_rows,
    value_rows,
    head_mixer,
    expand_weight,
    reduce_weight,
    cotangent,
):
    restored, grads = whole_step(
        token_ids.reshape(1, -1),
        embedding,
        queries,
        key_rows,
        value_rows,
        cotangent,
        head_mixer,
        expand_weight,
        reduce_weight,
    )
    return restored, grads[0], grads[1].T


def solution(mesh):
    return jax.shard_map(
        local,
        mesh=mesh,
        in_specs=(
            P(("dp", "blk", "wide")),
            P(),
            P(("dp", "blk", "wide"), None),
            P(("dp", "blk", "wide"), None),
            P(("dp", "blk", "wide"), None),
            P(),
            P(None, "wide"),
            P("wide", None),
            P(("dp", "blk", "wide"), None),
        ),
        out_specs=(
            P(("dp", "blk", "wide"), None),
            P(("dp", "blk"), "wide"),
            P(("dp", "wide"), "blk"),
        ),
        check_vma=False,
    )
```

time: 195 us -> 100 us (0.51)
  waiting for transfers between devices: 38.4 us -> 0 us
  starting transfers between devices: 33.7 us -> 0 us
  Pallas kernels: 71.6 us -> 96.8 us
  matrix products: 17 us -> 0 us
  between operations: 14.3 us -> 0.65 us
  local copies, waits for them, and re-layouts: 12.8 us -> 2.7 us
  other arithmetic: 6.28 us -> 0 us
    all_to_all x5 -> x0, waiting for transfers between devices: 38.3 us -> none  [the longest x2 24.6 us: copy_for_each(): return lax.all_to_all(copies, axis, split_axis=0, concat_axis=0, tiled=True)]
    pallas_call x1, Pallas kernels: 71.6 us -> 96.8 us  [whole_step(): pl.pallas_call(step_kernel, name='step', out_shape=(jax.ShapeDtypeStruct(...]
    all_to_all x5 -> x0, starting transfers between devices: 22.8 us -> none  [the longest x2 8.93 us: copy_for_each(): return lax.all_to_all(copies, axis, split_axis=0, concat_axis=0, tiled=True)]
    dot_general x9 -> x0, matrix products: 17 us -> none  [the longest x1 2.45 us: local(): jnp.dot(activated, reduce_weight, preferred_element_type=jnp.float32)]
    ppermute x3 -> x0, starting transfers between devices: 10.8 us -> none  [from_behind(): return lax.ppermute(array, axis, pairs)]
    all_to_all x2 -> x0, local copies, waits for them, and re-layouts: 4.44 us -> none  [local(): lax.all_to_all(grad_wide, 'blk', split_axis=1, concat_axis=0, tiled=True)]
    convert_element_type x5 -> x0, other arithmetic: 4.04 us -> none  [the longest x2 2.46 us: local(): normed = (pooled_float * lax.rsqrt(jnp.mean(pooled_float * pooled_float,...]
    convert_element_type x2 -> x0, local copies, waits for them, and re-layouts: 3.58 us -> none  [the longest x1 2.24 us: local(): normed = (pooled_float * lax.rsqrt(jnp.mean(pooled_float * pooled_float,...]
  transfers between devices with their start and end apart: 9 -> 0, of which waited for: 4 -> 0; matrix products, arithmetic and copies ran while one was open for 11% -> 0% of each run, Pallas kernels for 0% -> 0%
where the time goes in v3:
time: 100 us
  Pallas kernels  96.8 us (97%)
  local copies, waits for them, and re-layouts  2.7 us (3%)
    pallas_call x1, Pallas kernels, whole_step(): pl.pallas_call(step_kernel, name='step', out_shape=(jax.ShapeDtypeStruct(...  96.8 us

profile of v3, /device:TPU:1, one launch (start us, length us, event | category | flops | bytes accessed | tf_op | source)
XLA Modules:
  0.0 100.1 jit_solution(12473043712889744056)
XLA Ops:
  0.6 96.8 %step.1 = (bf16[128,1536]{1,0:T(8,128)(2,1)}, f32[2,192,384]{2,1,0:T(8,128)}) custom-call(s32[1,128]{1,0:T(1,128)} %bitcast.7, f32[6,1536]{1,0:T(8,128)} %emb_ref.1, bf16[128,768]{1,0:T(8,128)(2,1)} %q_ref.1, bf16[128,768]{1,0:T(8,128)(2,1)} %k_ref.1, bf16[128,768]{1,0:T(8,128)(2,1)} %v_ref.1, bf16[128,1536]{1,0:T(8,128)(2,1)} %cot_ref.1, ...), custom_call_target="tpu_custom_call" | custom-call | tf_op jit(solution)/shard_map/step/pallas_call | solution.py:793
  97.4 0.0 copy-start
  97.4 2.0 %slice_bitcast_fusion = (f32[384,192]{0,1:T(8,128)}, f32[192,384]{1,0:T(8,128)}) fusion(f32[2,192,384]{2,1,0:T(8,128)} %get-tuple-element.6), kind=kLoop, calls=%fused_computation | loop fusion | bytes 1179648 | tf_op jit(solution)/shard_map/transpose | solution.py:889
  99.4 0.0 copy-done
  99.4 0.7 copy.13
Async XLA Ops:
  97.4 2.0 %copy-start = (bf16[128,1536]{1,0:T(8,128)(2,1)S(1)}, bf16[128,1536]{1,0:T(8,128)(2,1)}, u32[]{:S(2)}) copy-start(bf16[128,1536]{1,0:T(8,128)(2,1)} %get-tuple-element.12) | copy-start | bytes 1179652

commit v4 on v3

--- a/solution.py
+++ b/solution.py
@@ -12,8 +12,9 @@
 
 MESH = pl.DeviceIdType.MESH
 ROUNDS = 8
-RELAY, ACROSS, LAST = 2, 3, 4
+RELAY, ACROSS, LAST = 2, 4, 5
 LEAD = 3
+GRADS = 5
 SCALE = HEAD ** (-0.5) * 1.4426950408889634
 MASKED = -2e38
 EMPTY = -1e30
@@ -39,15 +40,20 @@
 def step_kernel(
     tok_ref,
     emb_ref,
+    q_hbm,
+    k_hbm,
+    v_hbm,
+    cot_hbm,
+    mixer_hbm,
+    w1_hbm,
+    w2_hbm,
+    restored_ref,
+    expand_ref,
+    reduce_ref,
     q_ref,
     k_ref,
     v_ref,
     cot_ref,
-    mixer_hbm,
-    w1_hbm,
-    w2_hbm,
-    restored_ref,
-    grads_ref,
     qbuf,
     kvbuf,
     acc,
@@ -56,6 +62,8 @@
     pobuf,
     abuf,
     pst,
+    ph,
+    poh,
     mixer_ref,
     w1_ref,
     w2_ref,
@@ -85,10 +93,12 @@
     o_send,
     po_send,
     px_send,
+    pg_send,
     q_recv,
     kv_recv,
     o_recv,
     po_recv,
+    ph_recv,
     px_recv,
     row_send,
     row_recv,
@@ -141,7 +151,13 @@
             ((mixer_hbm, mixer_ref), (w1_hbm, w1_ref), (w2_hbm, w2_ref))
         )
     ]
-    for copy in weights_in:
+    rows_in = [
+        pltpu.make_async_copy(src, dst, w_sem.at[n + 3])
+        for n, (src, dst) in enumerate(
+            ((k_hbm, k_ref), (v_hbm, v_ref), (q_hbm, q_ref), (cot_hbm, cot_ref))
+        )
+    ]
+    for copy in rows_in:
         copy.start()
 
     def remote(src, dst, send, recv, where):
@@ -171,6 +187,7 @@
     inside = inside.astype(jnp.float32)
     after = jnp.where(own, (inside + 1.0) / 8, 0.0).astype(jnp.bfloat16)
     before = jnp.where(own, (7.0 - inside) / 8, 0.0).astype(jnp.bfloat16)
+    rows_in[3].wait()
     cot = cot_ref[...]
     later_part = jnp.dot(before, cot, preferred_element_type=jnp.float32)
     lbuf[:16] = later_part
@@ -190,8 +207,10 @@
 
     @pl.when(b == 0)
     def _():
-        pst[256:] = jnp.zeros((16, 768), jnp.bfloat16)
-
+        ph[256:] = jnp.zeros((16, HEAD), jnp.bfloat16)
+
+    for copy in rows_in[:3]:
+        copy.wait()
     pl.semaphore_wait(barrier, 14)
     mine = pl.ds(pl.multiple_of(z * 16, 16), 16)
 
@@ -315,6 +334,8 @@
     def _(j):
         greet(ready, {"blk": lax.rem(b + j, 8), "wide": z})
 
+    for copy in weights_in:
+        copy.start()
     pl.semaphore_wait(ready, 7)
     send_queries()
 
@@ -414,32 +435,34 @@
         return pltpu.make_async_copy(obuf.at[n], abuf.at[:, head_columns(z)], o_recv)
 
     def pool_target():
-        return pst.at[pl.ds(pl.multiple_of(home * 32, 32), 32), head_columns(z)]
-
-    def pool_copy(n, w):
+        return ph.at[pl.ds(pl.multiple_of(home * 32, 32), 32)]
+
+    def pool_copy(n):
         return remote(
-            pobuf.at[n], pool_target(), po_send.at[n, w], po_recv, {"blk": n, "wide": w}
+            pobuf.at[n], pool_target(), po_send.at[n], ph_recv, {"blk": n, "wide": z}
         )
 
     def pool_local(n):
-        return pltpu.make_async_copy(pobuf.at[n], pool_target(), po_recv)
-
-    def edge_copy(n, w):
+        return pltpu.make_async_copy(pobuf.at[n], pool_target(), ph_recv)
+
+    def edge_copy(n):
         return remote(
             pobuf.at[n, pl.ds(16, 16)],
-            pst.at[pl.ds(256, 16), head_columns(z)],
-            px_send.at[n, w],
+            ph.at[pl.ds(256, 16)],
+            px_send.at[n],
             px_recv,
-            {"blk": n + 1, "wide": w},
+            {"blk": n + 1, "wide": z},
         )
 
     def edge_local(n):
-        return pltpu.make_async_copy(
-            pobuf.at[n, pl.ds(16, 16)], pst.at[pl.ds(256, 16), head_columns(z)], px_recv
-        )
-
-    def is_next(n, w):
-        return jnp.logical_and(n + 1 == b, w == z)
+        return pltpu.make_async_copy(pobuf.at[n, pl.ds(16, 16)], ph.at[pl.ds(256, 16)], px_recv)
+
+    def spread_copy(j):
+        where = {"blk": b, "wide": lax.rem(z + j, 8)}
+        return remote(poh, pst.at[:, head_columns(z)], pg_send.at[j - 1], po_recv, where)
+
+    def spread_local():
+        return pltpu.make_async_copy(poh, pst.at[:, head_columns(z)], po_recv)
 
     @pl.when(z < FINE_HEADS)
     def _():
@@ -476,9 +499,12 @@
                 landed(piece(r, across), kv_recv.at[r, across])
                 opp_copy(r).start()
 
+            @pl.when(i == GRADS)
+            def _():
+                send_grads()
+
             @pl.when(i == LAST)
             def _():
-                send_grads()
                 for n in range(8):
                     landed(qbuf.at[n], q_recv.at[n])
 
@@ -504,28 +530,45 @@
             obuf[n] = out
             pobuf[n] = jnp.dot(pool, out, preferred_element_type=jnp.float32).astype(jnp.bfloat16)
 
-            @pl.loop(0, 8)
-            def _(w):
-                at_self = jnp.logical_and(n == b, w == z)
-
-                @pl.when(at_self)
+            @pl.when(n == b)
+            def _():
+                pool_local(n).start()
+
+            @pl.when(n != b)
+            def _():
+                pool_copy(n).start()
+
+            if n < 7:
+
+                @pl.when(jnp.logical_and(home == 7, n + 1 == b))
                 def _():
-                    pool_local(n).start()
-
-                @pl.when(jnp.logical_not(at_self))
+                    edge_local(n).start()
+
+                @pl.when(jnp.logical_and(home == 7, n + 1 != b))
                 def _():
-                    pool_copy(n, w).start()
-
-                if n < 7:
-                    crosses = home == 7
-
-                    @pl.when(jnp.logical_and(crosses, is_next(n, w)))
-                    def _():
-                        edge_local(n).start()
-
-                    @pl.when(jnp.logical_and(crosses, jnp.logical_not(is_next(n, w))))
-                    def _():
-                        edge_copy(n, w).start()
+                    edge_copy(n).start()
+
+        row = lax.broadcasted_iota(jnp.int32, (128, 272), 0)
+        col = lax.broadcasted_iota(jnp.int32, (128, 272), 1)
+        group = lax.shift_right_logical(row, 4)
+        within = jnp.bitwise_and(row, 15)
+        edge = jnp.where(group == 0, 256, 32 * group - 16)
+        picked = jnp.logical_or(
+            col == 32 * group + within, jnp.logical_and(within == 0, col == edge)
+        )
+        picked = jnp.where(picked, 1.0, 0.0).astype(jnp.bfloat16)
+
+        @pl.when(b > 0)
+        def _():
+            landed(ph.at[pl.ds(256, 16)], px_recv)
+
+        landed(ph.at[pl.ds(0, 256)], ph_recv)
+        poh[...] = jnp.dot(picked, ph[...], preferred_element_type=jnp.float32).astype(jnp.bfloat16)
+        spread_local().start()
+
+        @pl.loop(1, 8)
+        def _(j):
+            spread_copy(j).start()
 
         for n in range(8):
             here = jnp.logical_and(n == b, z == home)
@@ -586,23 +629,8 @@
         precision=lax.Precision.HIGHEST,
         preferred_element_type=jnp.float32,
     )
-    row = lax.broadcasted_iota(jnp.int32, (128, 272), 0)
-    col = lax.broadcasted_iota(jnp.int32, (128, 272), 1)
-    group = lax.shift_right_logical(row, 4)
-    within = jnp.bitwise_and(row, 15)
-    edge = jnp.where(group == 0, 256, 32 * group - 16)
-    picked = jnp.logical_or(
-        col == 32 * group + within, jnp.logical_and(within == 0, col == edge)
-    )
-    picked = jnp.where(picked, 1.0, 0.0).astype(jnp.bfloat16)
-
-    @pl.when(b > 0)
-    def _():
-        landed(pst.at[pl.ds(256, 16)], px_recv)
-
-    landed(pst.at[pl.ds(0, 256)], po_recv)
-    gathered = jnp.dot(picked, pst[...], preferred_element_type=jnp.float32).astype(jnp.bfloat16)
-    pooled = embedded + jnp.dot(gathered, mixer_ref[...], preferred_element_type=jnp.float32)
+    landed(pst, po_recv)
+    pooled = embedded + jnp.dot(pst[...], mixer_ref[...], preferred_element_type=jnp.float32)
     pooled = pooled.astype(jnp.bfloat16)
     pw[...] = pooled
     pooled_wide = pooled.astype(jnp.float32)
@@ -709,13 +737,13 @@
 
     @pl.when(odd == 0)
     def _():
-        grads_ref[0] = expanded[:192]
-        grads_ref[1] = reduced[:192]
+        expand_ref[...] = expanded[:192]
+        reduce_ref[...] = reduced[:192]
 
     @pl.when(odd == 1)
     def _():
-        grads_ref[0] = expanded[64:]
-        grads_ref[1] = reduced[64:]
+        expand_ref[...] = expanded[64:]
+        reduce_ref[...] = reduced[64:]
 
     @pl.when(holds_head)
     def _():
@@ -738,19 +766,17 @@
             def _():
                 o_copy(n).wait_send()
 
-            @pl.loop(0, 8)
-            def _(w):
-                @pl.when(jnp.logical_not(jnp.logical_and(n == b, w == z)))
-                def _():
-                    pool_copy(n, w).wait_send()
-
-                @pl.when(
-                    jnp.logical_and(
-                        jnp.logical_and(home == 7, n < 7), jnp.logical_not(is_next(n, w))
-                    )
-                )
-                def _():
-                    edge_copy(n, w).wait_send()
+            @pl.when(n != b)
+            def _():
+                pool_copy(n).wait_send()
+
+            @pl.when(jnp.logical_and(jnp.logical_and(home == 7, n < 7), n + 1 != b))
+            def _():
+                edge_copy(n).wait_send()
+
+        @pl.loop(1, 8)
+        def _(j):
+            spread_copy(j).wait_send()
 
     @pl.loop(0, FINE_HEADS)
     def _(h):
@@ -795,11 +821,16 @@
         name="step",
         out_shape=(
             jax.ShapeDtypeStruct((rows, 1536), bf16),
-            jax.ShapeDtypeStruct((2, 192, 384), f32),
+            jax.ShapeDtypeStruct((192, 384), f32),
+            jax.ShapeDtypeStruct((192, 384), f32),
         ),
-        in_specs=[vmem] * 6 + [hbm] * 3,
-        out_specs=(vmem, vmem),
+        in_specs=[vmem] * 2 + [hbm] * 7,
+        out_specs=(vmem,) * 3,
         scratch_shapes=[
+            pltpu.VMEM((rows, 768), bf16),
+            pltpu.VMEM((rows, 768), bf16),
+            pltpu.VMEM((rows, 768), bf16),
+            pltpu.VMEM((rows, 1536), bf16),
             pltpu.VMEM((8, rows, HEAD), bf16),
             pltpu.VMEM((ROUNDS, 2, 8, rows, HEAD), bf16),
             pltpu.VMEM((8, rows, 2 * HEAD), f32),
@@ -807,7 +838,9 @@
             pltpu.VMEM((8, rows, HEAD), bf16),
             pltpu.VMEM((8, 32, HEAD), bf16),
             pltpu.VMEM((rows, 768), bf16),
-            pltpu.VMEM((272, 768), bf16),
+            pltpu.VMEM((rows, 768), bf16),
+            pltpu.VMEM((272, HEAD), bf16),
+            pltpu.VMEM((rows, HEAD), bf16),
             pltpu.VMEM((768, 1536), bf16),
             pltpu.VMEM((1536, 384), bf16),
             pltpu.VMEM((384, 1536), bf16),
@@ -828,17 +861,19 @@
             pltpu.VMEM((8, 128, 256), bf16),
             pltpu.VMEM((128, 1536), f32),
             pltpu.SemaphoreType.REGULAR,
-            dma((3,)),
+            dma((7,)),
             dma((FINE_HEADS,)),
             dma((ROUNDS, 2)),
             dma((ROUNDS, 3)),
             dma((ROUNDS, 4)),
             dma((ROUNDS,)),
             dma((8,)),
-            dma((8, 8)),
-            dma((8, 8)),
+            dma((8,)),
+            dma((8,)),
+            dma((7,)),
             dma((8,)),
             dma((ROUNDS, 8)),
+            dma,
             dma,
             dma,
             dma,
@@ -875,7 +910,7 @@
     reduce_weight,
     cotangent,
 ):
-    restored, grads = whole_step(
+    restored, expand_grad, reduce_grad = whole_step(
         token_ids.reshape(1, -1),
         embedding,
         queries,
@@ -886,7 +921,7 @@
         expand_weight,
         reduce_weight,
     )
-    return restored, grads[0], grads[1].T
+    return restored, expand_grad, reduce_grad.T
 
 
 def solution(mesh):

time: 100 us -> 92.1 us (0.921)
  Pallas kernels: 96.8 us -> 87 us
  local copies, waits for them, and re-layouts: 2.7 us -> 4.22 us
    pallas_call x1, Pallas kernels: 96.8 us -> 87 us  [whole_step(): pl.pallas_call(step_kernel, name='step', out_shape=(jax.ShapeDtypeStruct(...]
    unnamed x3 -> x5, local copies, waits for them, and re-layouts: 0.75 us -> 4.22 us
    transpose x1 -> x0, local copies, waits for them, and re-layouts: 1.95 us -> none  [local(): return (restored, grads[0], grads[1].T)]
where the time goes in v4:
time: 92.1 us; the launch traced here: 91.9 us
  Pallas kernels  87 us (94%)
  local copies, waits for them, and re-layouts  4.22 us (5%)
    pallas_call x1, Pallas kernels, whole_step(): pl.pallas_call(step_kernel, name='step', out_shape=(jax.ShapeDtypeStruct(...  87 us
    unnamed x5, local copies, waits for them, and re-layouts  4.22 us

profile of v4, /device:TPU:1, one launch (start us, length us, event | category | flops | bytes accessed | tf_op | source)
XLA Modules:
  0.0 91.9 jit_solution(4299611885696805582)
XLA Ops:
  0.6 87.0 %step.1 = (bf16[128,1536]{1,0:T(8,128)(2,1)}, f32[192,384]{1,0:T(8,128)}, f32[192,384]{1,0:T(8,128)}) custom-call(s32[1,128]{1,0:T(1,128)} %bitcast.3, f32[6,1536]{1,0:T(8,128)} %emb_ref.1, bf16[128,768]{1,0:T(8,128)(2,1)} %q_hbm.1, bf16[128,768]{1,0:T(8,128)(2,1)} %k_hbm.1, bf16[128,768]{1,0:T(8,128)(2,1)} %v_hbm.1, bf16[128,1536]{1,0:T(8,128)(2,1)} %cot_hbm.1, ...), custom_call_target="tpu_custom_call" | custom-call | tf_op jit(solution)/shard_map/step/pallas_call | solution.py:819
  87.7 0.0 copy-start
  87.7 1.8 %copy.15 = bf16[128,1536]{1,0:T(8,128)(2,1)} copy(bf16[128,1536]{1,0:T(8,128)(2,1)} %get-tuple-element.12) | data formatting | bytes 786432
  89.5 1.7 %copy.16 = f32[192,384]{1,0:T(8,128)} copy(f32[192,384]{1,0:T(8,128)} %get-tuple-element.13) | data formatting | bytes 589824
  91.2 0.0 copy-done
  91.2 0.7 copy.17
Async XLA Ops:
  87.7 3.5 %copy-start = (f32[192,384]{1,0:T(8,128)S(1)}, f32[192,384]{1,0:T(8,128)}, u32[]{:S(2)}) copy-start(f32[192,384]{1,0:T(8,128)} %get-tuple-element.8) | copy-start | bytes 884740

commit v5 on v4

--- a/solution.py
+++ b/solution.py
@@ -396,30 +396,39 @@
 
     def compute(r):
         source = lax.rem(z + offset_of(r) + 8, 8)
-        rows = lax.broadcasted_iota(jnp.int32, (HEAD, HEAD), 0)
-        cols = lax.broadcasted_iota(jnp.int32, (HEAD, HEAD), 1)
-        allowed = cols + (source - home) * HEAD <= rows
-        for n in range(8):
-            keys = kvbuf[r, 0, : n + 1].reshape((n + 1) * HEAD, HEAD)
-            values = kvbuf[r, 1, : n + 1].reshape((n + 1) * HEAD, HEAD)
+        pair = 2 * HEAD
+        row = lax.broadcasted_iota(jnp.int32, (pair, pair), 0)
+        col = lax.broadcasted_iota(jnp.int32, (pair, pair), 1)
+        gap = col - row + 7 * HEAD * (
+            lax.shift_right_logical(col, 7) - lax.shift_right_logical(row, 7)
+        )
+        allowed = gap + (source - home) * HEAD <= 0
+        for n in range(0, 8, 2):
+            m = n + 2
+            keys = kvbuf[r, 0, :m].reshape(m * HEAD, HEAD)
+            values = kvbuf[r, 1, :m].reshape(m * HEAD, HEAD)
             scores = lax.dot_general(
-                qbuf[n], keys, (((1,), (1,)), ((), ())), preferred_element_type=jnp.float32
+                qbuf[n:m].reshape(pair, HEAD),
+                keys,
+                (((1,), (1,)), ((), ())),
+                preferred_element_type=jnp.float32,
             )
             last = jnp.where(allowed, scores[:, n * HEAD :], MASKED)
             if n:
                 scores = jnp.concatenate([scores[:, : n * HEAD], last], 1)
             else:
                 scores = last
-            before = maxima[n]
+            before = maxima[n:m].reshape(pair, HEAD)
             highest = jnp.maximum(before, scores.max(-1, keepdims=True) * SCALE)
-            weights = jnp.exp2(scores * SCALE - jnp.concatenate([highest] * (n + 1), 1))
+            weights = jnp.exp2(scores * SCALE - jnp.concatenate([highest] * m, 1))
             factor = jnp.exp2(before - highest)
             extended = jnp.concatenate([values, jnp.ones_like(values)], 1)
             summed = jnp.dot(
                 weights.astype(jnp.bfloat16), extended, preferred_element_type=jnp.float32
             )
-            acc[n] = acc[n] * jnp.concatenate([factor, factor], 1) + summed
-            maxima[n] = highest
+            held = acc[n:m].reshape(pair, pair) * jnp.concatenate([factor, factor], 1) + summed
+            acc[n:m] = held.reshape(2, HEAD, pair)
+            maxima[n:m] = highest.reshape(2, HEAD, HEAD)
 
     def o_copy(n):
         return pltpu.make_async_remote_copy(

time: 92.1 us -> 90.7 us (0.985)
  Pallas kernels: 87 us -> 85.6 us
    pallas_call x1, Pallas kernels: 87 us -> 85.6 us  [whole_step(): pl.pallas_call(step_kernel, name='step', out_shape=(jax.ShapeDtypeStruct(...]
where the time goes in v5:
time: 90.7 us; the launch traced here: 90.5 us
  Pallas kernels  85.6 us (94%)
  local copies, waits for them, and re-layouts  4.22 us (5%)
    pallas_call x1, Pallas kernels, whole_step(): pl.pallas_call(step_kernel, name='step', out_shape=(jax.ShapeDtypeStruct(...  85.6 us
    unnamed x5, local copies, waits for them, and re-layouts  4.22 us

profile of v5, /device:TPU:1, one launch (start us, length us, event | category | flops | bytes accessed | tf_op | source)
XLA Modules:
  0.0 90.5 jit_solution(14404045508673060286)
XLA Ops:
  0.6 85.6 %step.1 = (bf16[128,1536]{1,0:T(8,128)(2,1)}, f32[192,384]{1,0:T(8,128)}, f32[192,384]{1,0:T(8,128)}) custom-call(s32[1,128]{1,0:T(1,128)} %bitcast.3, f32[6,1536]{1,0:T(8,128)} %emb_ref.1, bf16[128,768]{1,0:T(8,128)(2,1)} %q_hbm.1, bf16[128,768]{1,0:T(8,128)(2,1)} %k_hbm.1, bf16[128,768]{1,0:T(8,128)(2,1)} %v_hbm.1, bf16[128,1536]{1,0:T(8,128)(2,1)} %cot_hbm.1, ...), custom_call_target="tpu_custom_call" | custom-call | tf_op jit(solution)/shard_map/step/pallas_call | solution.py:828
  86.3 0.0 copy-start
  86.3 1.8 %copy.15 = bf16[128,1536]{1,0:T(8,128)(2,1)} copy(bf16[128,1536]{1,0:T(8,128)(2,1)} %get-tuple-element.12) | data formatting | bytes 786432
  88.1 1.7 %copy.16 = f32[192,384]{1,0:T(8,128)} copy(f32[192,384]{1,0:T(8,128)} %get-tuple-element.13) | data formatting | bytes 589824
  89.8 0.0 copy-done
  89.8 0.7 copy.17
Async XLA Ops:
  86.3 3.5 %copy-start = (f32[192,384]{1,0:T(8,128)S(1)}, f32[192,384]{1,0:T(8,128)}, u32[]{:S(2)}) copy-start(f32[192,384]{1,0:T(8,128)} %get-tuple-element.8) | copy-start | bytes 884740
